TPU v7x, 512 devices: a whole 4x8x8 slice. The times are simulated.
512 devices in a mesh: blk: 64 (over x, y, core), body: 8 (over z).
Axes of the slice: x: 4, y: 8, z: 8, core: 2. Of those that a mesh axis runs over, the one named last changes fastest.
Arguments:
- positions: float32 [3, 1048576], P(None, ('blk', 'body')), may hold values from -2.5 to 2.5
- direction: float32 [3, 1048576], P(None, ('blk', 'body')), may hold values from -6 to 6
- pair_local: int32 [32768], P(('blk', 'body')), may hold values from 0 to 15
- pair_peer: int32 [32768], P(('blk', 'body')), may hold values from 0 to 63, as said below
- pair_shift: int32 [32768], P(('blk', 'body')), may hold values from 1 to 15
- pair_count: int32 [512], P(('blk', 'body')), may hold values from 32 to 64, as said below
- face_index: int32 [2048], P(('blk', 'body')), may hold values from 0 to 15
- cross_local: int32 [4096], P(('blk', 'body')), may hold values from 0 to 15
- cross_face: int32 [4096], P(('blk', 'body')), may hold values from 0 to 3
Outputs:
- gradient: float32 [3, 1048576], P(None, ('blk', 'body'))
- hess_dir: float32 [3, 1048576], P(None, ('blk', 'body'))
Inputs may be any that keep to these rules, and one draw needn't show every extreme that they name: `pair_peer`: among the 64 slots of one device, used or not, at most 2 name the same peer; in every draw some device has 2 slots naming one peer. `pair_count`: some device uses all 64 slots.
All inputs are finite; a program needn't handle non-finite values.
Results may differ from a plain program's by a relative error of at most 0.0003.
Values sent between devices are 32-bit elements; how exact they have to be, the bound alone decides.
No kernel may reach another device: no remote copies, remote signals or barrier semaphores. Data moves between devices by JAX's collectives and lax.ppermute only.
A program may use at most 64 MiB of HBM per device.

v0:
```python
import jax
import jax.numpy as jnp
from jax import lax
from jax.experimental import pallas as pl
from jax.experimental.pallas import tpu as pltpu
from jax.sharding import PartitionSpec as P

XI = 0.1
SCALE = -0.04
GROUP = 4
LANES = 128
MSG = 13
RET = 12
F32 = jnp.float32
BF16 = jnp.bfloat16
NN = (((1,), (0,)), ((), ()))
NT = (((1,), (1,)), ((), ()))


def from_behind(value, axis, steps):
    count = lax.axis_size(axis)
    first, last = (max(0, -steps), min(count, count - steps))
    return lax.ppermute(value, axis, [(source, source + steps) for source in range(first, last)])


def block_rows(pos_ref, dir_ref, block):
    cols = pl.ds(pl.multiple_of(block * LANES, LANES), LANES)
    return pos_ref[:, cols], dir_ref[:, cols]


def pack_kernel(
    local_ref, peer_ref, shift_ref, count_ref, face_ref, pos_ref, dir_ref,
    send_ref, faces_ref, slot_ref, used_ref,
):
    peers = used_ref.shape[0]
    num_blocks = pos_ref.shape[1] // LANES
    lane = lax.broadcasted_iota(jnp.int32, (1, LANES), 1)
    unused = jnp.full((1, LANES), -1.0, F32)
    for face in range(face_ref.shape[0]):
        near_pos, near_dir = block_rows(pos_ref, dir_ref, face_ref[face])
        faces_ref[face * 6 : face * 6 + 3, :] = near_pos
        faces_ref[face * 6 + 3 : face * 6 + 6, :] = near_dir
    for peer in range(peers):
        used_ref[peer] = 0
        row = peer * MSG + RET
        send_ref[row : row + 1, :] = unused

    def one(pair, carry):
        near = local_ref[pair]
        peer = peer_ref[pair]
        far = lax.rem(near + shift_ref[pair], num_blocks)
        rank = used_ref[peer]
        used_ref[peer] = rank + 1
        slot_ref[pair] = peer * RET + rank * 6
        near_pos, near_dir = block_rows(pos_ref, dir_ref, near)
        base = peer * MSG
        send_ref[pl.ds(base + rank * 6, 3), :] = near_pos
        send_ref[pl.ds(base + rank * 6 + 3, 3), :] = near_dir
        row = pl.ds(base + RET, 1)
        send_ref[row, :] = jnp.where(lane == rank, far.astype(F32), send_ref[row, :])
        return carry

    lax.fori_loop(0, count_ref[0], one, 0)


def pieces(value):
    high = value.astype(BF16).astype(F32)
    rest = value - high
    mid = rest.astype(BF16).astype(F32)
    return high, mid, rest - mid


def own_terms(rows, sums):
    row = lax.broadcasted_iota(jnp.int32, (8, LANES), 0)
    by_grad = sums[:, :LANES]
    by_curv = sums[:, LANES:]
    first = rows * by_grad[6:7, :] - by_grad
    second = rows * by_curv[6:7, :] - by_curv
    shifted = pltpu.roll(second, 3, 0)
    return SCALE * (first + jnp.where((row >= 3) & (row < 6), shifted, 0.0))


def fold(product):
    return product[0:8] + product[8:16] + product[16:24]


def stacked(rows):
    row = lax.broadcasted_iota(jnp.int32, (8, LANES), 0)
    high, mid, low = pieces(jnp.where(row < 6, rows, jnp.where(row == 6, 1.0, 0.0)))
    tall = jnp.concatenate([high, mid, low, jnp.zeros_like(low)], axis=0).astype(BF16)
    return jnp.concatenate([tall, tall], axis=1)


def local_setup(pos_ref, dir_ref, rows_ref, feature_ref, left_ref, center_ref):
    row = lax.broadcasted_iota(jnp.int32, (8, LANES), 0)
    for block in range(pos_ref.shape[1] // LANES):
        span = slice(block * LANES, (block + 1) * LANES)
        rows = jnp.concatenate(
            [pos_ref[:, span], dir_ref[:, span], jnp.zeros((2, LANES), F32)], axis=0
        )
        center = jnp.mean(rows, axis=1, keepdims=True)
        rows = rows - center
        center_ref[block] = jnp.broadcast_to(center, (8, LANES))
        rows_ref[block] = jnp.where(row == 6, 1.0, rows)
        left_ref[block] = stacked(rows)
        square = jnp.sum(rows[0:3] * rows[0:3], axis=0, keepdims=True)
        cross = jnp.sum(rows[0:3] * rows[3:6], axis=0, keepdims=True)
        full = jnp.where(row == 6, square, jnp.where(row == 7, cross + cross, rows))
        high, mid, low = pieces(full)
        one = jnp.ones_like(full)
        feature_ref[block] = jnp.concatenate(
            [high, high, mid, high, mid, low, one, jnp.zeros_like(one)], axis=0
        ).T.astype(BF16)


def remote_feature(rows):
    row = lax.broadcasted_iota(jnp.int32, (8, LANES), 0)
    twice = -2.0 * rows
    for_square = jnp.where(row < 3, twice, jnp.where(row == 6, 1.0, 0.0))
    swapped = jnp.where(row < 3, pltpu.roll(twice, 5, 0), pltpu.roll(twice, 3, 0))
    for_cross = jnp.where(row < 6, swapped, jnp.where(row == 7, 1.0, 0.0))
    square = jnp.sum(rows[0:3] * rows[0:3], axis=0, keepdims=True) + XI
    cross = jnp.sum(rows[0:3] * twice[3:6], axis=0, keepdims=True)
    high, mid, low = pieces(jnp.concatenate([for_square, for_cross], axis=1))
    own = jnp.concatenate([square, -cross], axis=1)
    own_high, own_mid, own_low = pieces(own)
    wide_row = lax.broadcasted_iota(jnp.int32, (8, 2 * LANES), 0)
    norms = jnp.where(
        wide_row == 0, own_high,
        jnp.where(wide_row == 1, own_mid, jnp.where(wide_row == 2, own_low, 0.0)),
    )
    return jnp.concatenate(
        [high, mid, high, low, mid, high, norms, jnp.zeros_like(norms)], axis=0
    ).astype(BF16)


def split(value):
    high = value.astype(BF16)
    return high, (value - high.astype(F32)).astype(BF16)


def pair_group(blocks, remotes, feature_ref, left_ref, center_ref):
    remotes = [remote - center_ref[block] for block, remote in zip(blocks, remotes)]
    both = [
        lax.dot_general(
            feature_ref[block], remote_feature(remote), NN, preferred_element_type=F32
        )
        for block, remote in zip(blocks, remotes)
    ]
    results = []
    row = lax.broadcasted_iota(jnp.int32, (8, LANES), 0)
    for block, remote, product in zip(blocks, remotes, both):
        squared = jnp.minimum(product[:, :LANES], 1.0)
        along = product[:, LANES:]
        log_twice = 2.0 * jnp.log(squared)
        excess = squared - 1.0
        ratio = excess / squared
        grad_high, grad_low = split(excess * (log_twice + ratio))
        curv_high, curv_low = split((log_twice + ratio * (4.0 - ratio)) * along)
        by_local = jnp.concatenate(
            [
                jnp.concatenate([grad_high, curv_high], axis=1),
                jnp.concatenate([grad_low, curv_low], axis=1),
            ],
            axis=0,
        )
        by_remote = jnp.concatenate(
            [
                jnp.concatenate([grad_high, grad_low], axis=1),
                jnp.concatenate([curv_high, curv_low], axis=1),
            ],
            axis=0,
        )
        for_remote = lax.dot_general(left_ref[block], by_local, NN, preferred_element_type=F32)
        for_local = lax.dot_general(stacked(remote), by_remote, NT, preferred_element_type=F32)
        remote_rows = jnp.where(row == 6, 1.0, remote)
        results.append((own_terms(remote_rows, fold(for_remote)), fold(for_local)))
    return results


def eight_rows(six):
    return jnp.concatenate([six, jnp.zeros((2, LANES), F32)], axis=0)


def cross_kernel(
    local_ref, face_ref, pos_ref, dir_ref, incoming_ref,
    sums_ref, back_ref, rows_ref, feature_ref, left_ref, center_ref,
):
    local_setup(pos_ref, dir_ref, rows_ref, feature_ref, left_ref, center_ref)
    sums_ref[...] = jnp.zeros_like(sums_ref)
    back_ref[...] = jnp.zeros_like(back_ref)

    def some(step, carry):
        pairs = [step * GROUP + k for k in range(GROUP)]
        blocks = [local_ref[pair] for pair in pairs]
        rows = [pl.ds(face_ref[pair] * 6, 6) for pair in pairs]
        remotes = [eight_rows(incoming_ref[row, :]) for row in rows]
        results = pair_group(blocks, remotes, feature_ref, left_ref, center_ref)
        for block, row, (remote, local) in zip(blocks, rows, results):
            back_ref[row, :] += remote[:6]
            sums_ref[block] += local
        return carry

    count = jnp.where(lax.axis_index("body") > 0, local_ref.shape[0] // GROUP, 0)
    lax.fori_loop(0, count, some, 0)


def main_kernel(
    arrived_ref, sums_in_ref, rows_ref, feature_ref, left_ref, center_ref,
    return_ref, terms_ref,
    sums_ref, list_ref, table_ref, sem,
):
    peers = arrived_ref.shape[0] // MSG
    marks = arrived_ref[pl.ds(RET, peers, stride=MSG), :].astype(BF16)
    pick = (
        lax.broadcasted_iota(jnp.int32, (16, LANES), 0)
        == lax.broadcasted_iota(jnp.int32, (16, LANES), 1)
    ).astype(BF16)
    found = lax.dot_general(pick, marks, NT, preferred_element_type=F32)
    wide = jnp.concatenate([found[0:1], found[1:2]], axis=1)
    slots = 2 * peers
    valid = wide >= 0.0
    slot = lax.broadcasted_iota(jnp.int32, (1, slots), 1)
    before = (
        lax.broadcasted_iota(jnp.int32, (slots, slots), 0)
        < lax.broadcasted_iota(jnp.int32, (slots, slots), 1)
    ).astype(BF16)
    ones = jnp.broadcast_to(valid.astype(F32), (16, slots)).astype(BF16)
    place = lax.dot_general(ones, before, NN, preferred_element_type=F32)[0:1]
    hot = (lax.broadcasted_iota(jnp.int32, (slots, slots), 0).astype(F32) == place) & valid
    row = lax.broadcasted_iota(jnp.int32, (16, slots), 0)
    codes = jnp.where(
        row == 0,
        jnp.broadcast_to(wide, (16, slots)),
        jnp.where(row == 1, jnp.broadcast_to(slot, (16, slots)).astype(F32), 0.0),
    ).astype(BF16)
    ordered = lax.dot_general(codes, hot.astype(F32).astype(BF16), NT, preferred_element_type=F32)
    total = jnp.sum(valid.astype(F32), axis=1, keepdims=True)
    ordered = jnp.where(
        lax.broadcasted_iota(jnp.int32, (8, slots), 0) == 2, total, ordered[:8]
    )
    list_ref[:, :slots] = ordered.astype(jnp.int32)
    copy = pltpu.make_async_copy(list_ref, table_ref, sem)
    copy.start()
    num_blocks = terms_ref.shape[0]
    sums_ref[0:num_blocks] = sums_in_ref[...]
    sums_ref[num_blocks] = jnp.zeros((8, 2 * LANES), F32)
    copy.wait()
    count = table_ref[2, 0]

    def some(step, carry):
        blocks, targets, remotes, rows = [], [], [], []
        for k in range(GROUP):
            pair = step * GROUP + k
            listed = jnp.minimum(pair, count - 1)
            block = table_ref[0, listed]
            where = table_ref[1, listed]
            second = (where >= peers).astype(jnp.int32)
            peer = where - second * peers
            blocks.append(block)
            targets.append(jnp.where(pair < count, block, num_blocks))
            remotes.append(eight_rows(arrived_ref[pl.ds(peer * MSG + second * 6, 6), :]))
            rows.append(pl.ds(peer * RET + second * 6, 6))
        results = pair_group(blocks, remotes, feature_ref, left_ref, center_ref)
        for target, row, (remote, local) in zip(targets, rows, results):
            return_ref[row, :] = remote[:6]
            sums_ref[target] += local
        return carry

    lax.fori_loop(0, (count + GROUP - 1) // GROUP, some, 0)
    for block in range(terms_ref.shape[0]):
        terms_ref[block] = own_terms(rows_ref[block], sums_ref[block])


def finish_kernel(
    local_ref, slot_ref, count_ref, face_ref, returned_ref, terms_ref, back_ref,
    grad_ref, hess_ref,
    total_ref,
):
    total_ref[...] = terms_ref[...]
    for face in range(face_ref.shape[0]):
        total_ref[face_ref[face], 0:6, :] += back_ref[face * 6 : face * 6 + 6, :]

    def one(pair, carry):
        total_ref[local_ref[pair], 0:6, :] += returned_ref[pl.ds(slot_ref[pair], 6), :]
        return carry

    lax.fori_loop(0, count_ref[0], one, 0)
    for block in range(terms_ref.shape[0]):
        span = slice(block * LANES, (block + 1) * LANES)
        grad_ref[:, span] = total_ref[block, 0:3, :]
        hess_ref[:, span] = total_ref[block, 3:6, :]


def smem():
    return pl.BlockSpec(memory_space=pltpu.SMEM)


def vmem():
    return pl.BlockSpec(memory_space=pltpu.VMEM)


def on_chip(*shape, dtype=F32):
    return pltpu.VMEM(shape, dtype)


def held(*values):
    return [pltpu.with_memory_space_constraint(value, pltpu.VMEM) for value in values]


def per_device(
    positions, direction, pair_local, pair_peer, pair_shift, pair_count,
    face_index, cross_local, cross_face,
):
    num_blocks = positions.shape[1] // LANES
    peers = lax.axis_size("blk")
    faces = face_index.shape[0]
    setup = (
        on_chip(num_blocks, 8, LANES),
        on_chip(num_blocks, LANES, 64, dtype=BF16),
        on_chip(num_blocks, 32, 2 * LANES, dtype=BF16),
        on_chip(num_blocks, 8, LANES),
    )
    send, face_rows, slots = pl.pallas_call(
        pack_kernel,
        name="pack",
        out_shape=(
            on_chip(peers * MSG, LANES),
            on_chip(faces * 6, LANES),
            pltpu.SMEM((pair_local.shape[0],), jnp.int32),
        ),
        in_specs=[smem()] * 5 + [vmem()] * 2,
        out_specs=(vmem(), vmem(), smem()),
        scratch_shapes=[pltpu.SMEM((peers,), jnp.int32)],
    )(pair_local, pair_peer, pair_shift, pair_count, face_index, positions, direction)
    arrived = lax.all_to_all(
        send.reshape(peers, MSG, 1, LANES), "blk", split_axis=0, concat_axis=0, tiled=True
    ).reshape(peers * MSG, LANES)
    incoming = from_behind(face_rows, "body", 1)
    sums, back, *local = pl.pallas_call(
        cross_kernel,
        name="cross",
        out_shape=(on_chip(num_blocks, 8, 2 * LANES), on_chip(faces * 6, LANES)) + setup,
        in_specs=[smem()] * 2 + [vmem()] * 3,
        out_specs=(vmem(),) * 6,
    )(cross_local, cross_face, positions, direction, *held(incoming))
    face_back = from_behind(back, "body", -1)
    outgoing, terms = pl.pallas_call(
        main_kernel,
        name="pairs",
        out_shape=(on_chip(peers * RET, LANES), on_chip(num_blocks, 8, LANES)),
        in_specs=[vmem()] * 6,
        out_specs=(vmem(), vmem()),
        scratch_shapes=[
            pltpu.VMEM((num_blocks + 1, 8, 2 * LANES), F32),
            pltpu.VMEM((8, LANES), jnp.int32),
            pltpu.SMEM((8, LANES), jnp.int32),
            pltpu.SemaphoreType.DMA,
        ],
    )(*held(arrived, sums, *local))
    returned = lax.all_to_all(
        outgoing.reshape(peers, RET, 1, LANES), "blk", split_axis=0, concat_axis=0, tiled=True
    ).reshape(peers * RET, LANES)
    return pl.pallas_call(
        finish_kernel,
        name="finish",
        out_shape=[jax.ShapeDtypeStruct((3, num_blocks * LANES), F32)] * 2,
        in_specs=[smem()] * 4 + [vmem()] * 3,
        out_specs=(vmem(), vmem()),
        scratch_shapes=[pltpu.VMEM((num_blocks, 8, LANES), F32)],
    )(pair_local, slots, pair_count, face_index, *held(returned, terms, face_back))


def solution(mesh):
    split = P(("blk", "body"))
    wide = P(None, ("blk", "body"))
    return jax.shard_map(
        per_device,
        mesh=mesh,
        in_specs=(wide, wide) + (split,) * 7,
        out_specs=(wide, wide),
        check_vma=False,
    )
```

profile of v0, /device:TPU:1, one launch (start us, length us, event | category | flops | bytes accessed | tf_op | source)
XLA Modules:
  0.0 63.1 jit_solution(15416585350157290554)
XLA Ops:
  1.3 2.1 %pack.1 = (f32[832,128]{1,0:T(8,128)}, f32[24,128]{1,0:T(8,128)S(1)}, s32[64]{0:T(128)S(4)}) custom-call(s32[64]{0:T(128)} %local_ref.5, s32[64]{0:T(128)} %peer_ref.1, s32[64]{0:T(128)} %shift_ref.1, s32[1]{0:T(128)S(6)} %copy.13.count_ref, s32[4]{0:T(128)} %face_ref.5, f32[3,2048]{1,0:T(4,128)} %pos_ref.3, f32[3,2048]{1,0:T(4,128)} %dir_ref.3), custom_call_target="tpu_custom_call" | custom-call | tf_op jit(solution)/shard_map/pack/pallas_call | solution.py:324
  3.4 11.7 %all-to-all-start = ((f32[64,13,1,128]{3,2,1,0:T(1,128)}), f32[64,13,1,128]{3,2,1,0:T(1,128)S(1)}, u32[]{:S(2)}, u32[]{:S(2)}) async-start(f32[64,13,1,128]{3,2,1,0:T(1,128)} %bitcast), calls=%async_computation | async-start | bytes 851968 | tf_op jit(solution)/shard_map/all_to_all | solution.py:336
  15.1 4.0 %collective-permute-start = (f32[24,128]{1,0:T(8,128)S(1)}, f32[24,128]{1,0:T(8,128)S(1)}, u32[]{:S(2)}, u32[]{:S(2)}) collective-permute-start(f32[24,128]{1,0:T(8,128)S(1)} %get-tuple-element.15), channel_id=1, source_target_pairs={{0,1},{1,2},{2,3},{3,4},{4,5},{5,6},{6,7},{8,9},{9,10},{10,11},{11... | collective-permute-start | bytes 36872 | tf_op jit(solution)/shard_map/ppermute | solution.py:23
  19.0 0.8 %collective-permute-done.incoming_ref = f32[24,128]{1,0:T(8,128)S(1)} collective-permute-done((f32[24,128]{1,0:T(8,128)S(1)}, f32[24,128]{1,0:T(8,128)S(1)}, u32[]{:S(2)}, u32[]{:S(2)}) %collective-permute-start) | collective-permute-done | bytes 12320 | tf_op jit(solution)/shard_map/ppermute | solution.py:23
  19.9 1.2 %cross.1 = (f32[16,8,256]{2,1,0:T(8,128)S(1)}, f32[24,128]{1,0:T(8,128)S(1)}, f32[16,8,128]{2,1,0:T(8,128)S(1)}, bf16[16,128,64]{2,1,0:T(8,128)(2,1)S(1)}, bf16[...) custom-call(s32[8]{0:T(128)} %local_ref.4, s32[8]{0:T(128)} %face_ref.4, f32[3,2048]{1,0:T(4,128)} %pos_ref.3, ...), custom_call_target="tpu_custom_call" | custom-call | tf_op jit(solution)/shard_map/cross/pallas_call | solution.py:340
  21.1 9.3 %all-to-all-done = f32[64,13,1,128]{3,2,1,0:T(1,128)S(1)} async-done(((f32[64,13,1,128]{3,2,1,0:T(1,128)}), f32[64,13,1,128]{3,2,1,0:T(1,128)S(1)}, u32[]{:S(2)}, u32[]{:S(2)}) %all-to-all-start) | async-done | bytes 426016 | tf_op jit(solution)/shard_map/all_to_all | solution.py:336
  30.4 7.6 %pairs.1 = (f32[768,128]{1,0:T(8,128)}, f32[16,8,128]{2,1,0:T(8,128)S(1)}) custom-call(f32[832,128]{1,0:T(8,128)S(1)} %bitcast.4, f32[16,8,256]{2,1,0:T(8,128)S(1)} %get-tuple-element.16.sums_in_ref, f32[16,8,128]{2,1,0:T(8,128)S(1)} %get-tuple-element.17.rows_ref, bf16[16,128,64]{2,1,0:T(8,128)(2,1)S(1)} %get-tuple-element.18.feature_ref, ...), custom_call_target="tpu_custom_call" | custom-call | tf_op jit(solution)/shard_map/pairs/pallas_call | solution.py:348
  38.0 9.0 %all-to-all-start.1 = ((f32[64,12,1,128]{3,2,1,0:T(1,128)}), f32[64,12,1,128]{3,2,1,0:T(1,128)S(1)}, u32[]{:S(2)}, u32[]{:S(2)}) async-start(f32[64,12,1,128]{3,2,1,0:T(1,128)} %bitcast.2), calls=%async_computation.1 | async-start | bytes 786432 | tf_op jit(solution)/shard_map/all_to_all | solution.py:361
  47.0 1.3 %collective-permute-start.1 = (f32[24,128]{1,0:T(8,128)S(1)}, f32[24,128]{1,0:T(8,128)S(1)}, u32[]{:S(2)}, u32[]{:S(2)}) collective-permute-start(f32[24,128]{1,0:T(8,128)S(1)} %get-tuple-element.23), channel_id=1, source_target_pairs={{1,0},{2,1},{3,2},{4,3},{5,4},{6,5},{7,6},{9,8},{10,9},{11,10},{12... | collective-permute-start | bytes 36872 | tf_op jit(solution)/shard_map/ppermute | solution.py:23
  48.3 3.4 %collective-permute-done.1.back_ref = f32[24,128]{1,0:T(8,128)S(1)} collective-permute-done((f32[24,128]{1,0:T(8,128)S(1)}, f32[24,128]{1,0:T(8,128)S(1)}, u32[]{:S(2)}, u32[]{:S(2)}) %collective-permute-start.1) | collective-permute-done | bytes 12320 | tf_op jit(solution)/shard_map/ppermute | solution.py:23
  51.7 9.8 %all-to-all-done.1 = f32[64,12,1,128]{3,2,1,0:T(1,128)S(1)} async-done(((f32[64,12,1,128]{3,2,1,0:T(1,128)}), f32[64,12,1,128]{3,2,1,0:T(1,128)S(1)}, u32[]{:S(2)}, u32[]{:S(2)}) %all-to-all-start.1) | async-done | bytes 393248 | tf_op jit(solution)/shard_map/all_to_all | solution.py:361
  61.5 1.6 %finish.1 = (f32[3,2048]{1,0:T(4,128)}, f32[3,2048]{1,0:T(4,128)}) custom-call(s32[64]{0:T(128)} %local_ref.5, s32[64]{0:T(128)S(4)} %get-tuple-element.13.slot_ref, s32[1]{0:T(128)S(6)} %copy.13.count_ref, s32[4]{0:T(128)} %face_ref.5, f32[768,128]{1,0:T(8,128)S(1)} %bitcast.5, f32[16,8,128]{2,1,0:T(8,128)S(1)} %get-tuple-element.22.terms_ref, ...), custom_call_target="tpu_custom_call" | custom-call | tf_op jit(solution)/shard_map/finish/pallas_call | solution.py:364
Async XLA Ops:
  3.4 27.0 %all-to-all-start = ((f32[64,13,1,128]{3,2,1,0:T(1,128)}), f32[64,13,1,128]{3,2,1,0:T(1,128)S(1)}, u32[]{:S(2)}, u32[]{:S(2)}) async-start(f32[64,13,1,128]{3,2,1,0:T(1,128)} %bitcast), calls=%async_computation | async-start | bytes 851968 | tf_op jit(solution)/shard_map/all_to_all | solution.py:336
  15.1 4.8 %collective-permute-start = (f32[24,128]{1,0:T(8,128)S(1)}, f32[24,128]{1,0:T(8,128)S(1)}, u32[]{:S(2)}, u32[]{:S(2)}) collective-permute-start(f32[24,128]{1,0:T(8,128)S(1)} %get-tuple-element.15), channel_id=1, source_target_pairs={{0,1},{1,2},{2,3},{3,4},{4,5},{5,6},{6,7},{8,9},{9,10},{10,11},{11... | collective-permute-start | bytes 36872 | tf_op jit(solution)/shard_map/ppermute | solution.py:23
  38.0 23.6 %all-to-all-start.1 = ((f32[64,12,1,128]{3,2,1,0:T(1,128)}), f32[64,12,1,128]{3,2,1,0:T(1,128)S(1)}, u32[]{:S(2)}, u32[]{:S(2)}) async-start(f32[64,12,1,128]{3,2,1,0:T(1,128)} %bitcast.2), calls=%async_computation.1 | async-start | bytes 786432 | tf_op jit(solution)/shard_map/all_to_all | solution.py:361
  47.0 4.7 %collective-permute-start.1 = (f32[24,128]{1,0:T(8,128)S(1)}, f32[24,128]{1,0:T(8,128)S(1)}, u32[]{:S(2)}, u32[]{:S(2)}) collective-permute-start(f32[24,128]{1,0:T(8,128)S(1)} %get-tuple-element.23), channel_id=1, source_target_pairs={{1,0},{2,1},{3,2},{4,3},{5,4},{6,5},{7,6},{9,8},{10,9},{11,10},{12... | collective-permute-start | bytes 36872 | tf_op jit(solution)/shard_map/ppermute | solution.py:23
where the time goes:
time: 62.7 us; the launch traced here: 63.1 us
  starting transfers between devices  26 us (41%)
  waiting for transfers between devices  23.3 us (37%)
  Pallas kernels  12.4 us (20%)
  between operations  1.32 us (2%)
    all_to_all x1, starting transfers between devices, per_device(): lax.all_to_all(send.reshape(peers, MSG, 1, LANES), 'blk', split_axis=0, c...  11.7 us
    all_to_all x1, waiting for transfers between devices, per_device(): lax.all_to_all(outgoing.reshape(peers, RET, 1, LANES), 'blk', split_axis=...  9.82 us
    all_to_all x1, waiting for transfers between devices, per_device(): lax.all_to_all(send.reshape(peers, MSG, 1, LANES), 'blk', split_axis=0, c...  9.27 us
    all_to_all x1, starting transfers between devices, per_device(): lax.all_to_all(outgoing.reshape(peers, RET, 1, LANES), 'blk', split_axis=...  9.04 us
    pallas_call x1, Pallas kernels, per_device(): pl.pallas_call(main_kernel, name='pairs', out_shape=(on_chip(peers * RET,...  7.59 us
    ppermute x2, starting transfers between devices, from_behind(): lax.ppermute(value, axis, [(source, source + steps) for source in range(f...  5.25 us
    ppermute x2, waiting for transfers between devices, from_behind(): lax.ppermute(value, axis, [(source, source + steps) for source in range(f...  4.25 us
    pallas_call x1, Pallas kernels, per_device(): pl.pallas_call(pack_kernel, name='pack', out_shape=(on_chip(peers * MSG,...  2.08 us
  transfers between devices with their start and end apart: 4, of which 4 were waited for; matrix products, arithmetic and copies ran while one was open for 0% of the time, Pallas kernels for 2%

commit v1 on v0

v1 whole, which is shorter than its diff:
```python
import jax
import jax.numpy as jnp
from jax import lax
from jax.experimental import pallas as pl
from jax.experimental.pallas import tpu as pltpu
from jax.sharding import PartitionSpec as P

XI = 0.1
SCALE = 0.02
LANES = 128
SIX = 6
MSG = 13
RET = 12
GROUP = 3
UNROLL = 4
F32 = jnp.float32
BF16 = jnp.bfloat16
NN = (((1,), (0,)), ((), ()))
NT = (((1,), (1,)), ((), ()))


def from_behind(value, axis, steps):
    count = lax.axis_size(axis)
    first, last = (max(0, -steps), min(count, count - steps))
    return lax.ppermute(value, axis, [(source, source + steps) for source in range(first, last)])


def put_block(target_ref, start, pos_ref, dir_ref, block):
    cols = pl.ds(pl.multiple_of(block * LANES, LANES), LANES)
    target_ref[pl.ds(start, 3), :] = pos_ref[:, cols]
    target_ref[pl.ds(start + 3, 3), :] = dir_ref[:, cols]


def pack_kernel(
    local_ref, peer_ref, shift_ref, count_ref, face_ref, pos_ref, dir_ref,
    send_ref, faces_ref, plan_ref, used_ref,
):
    peers = used_ref.shape[0]
    pairs = local_ref.shape[0]
    num_blocks = pos_ref.shape[1] // LANES
    count = count_ref[0]
    lane = lax.broadcasted_iota(jnp.int32, (1, LANES), 1)
    unused = jnp.full((1, LANES), -1.0, F32)
    for peer in range(peers):
        used_ref[peer] = 0
        row = peer * MSG + RET
        send_ref[row : row + 1, :] = unused

    def some(step, carry):
        for k in range(UNROLL):
            pair = step * UNROLL + k
            near = local_ref[pair]
            peer = peer_ref[pair]
            far = lax.rem(near + shift_ref[pair], num_blocks)
            mark = jnp.where(pair < count, far, -1).astype(F32)
            rank = used_ref[peer]
            used_ref[peer] = rank + 1
            plan_ref[pair] = peer * RET + rank * SIX
            plan_ref[pairs + pair] = near
            put_block(send_ref, peer * MSG + rank * SIX, pos_ref, dir_ref, near)
            pltpu.store(
                send_ref.at[pl.ds(peer * MSG + RET, 1), :],
                jnp.broadcast_to(mark, (1, LANES)),
                mask=lane == rank,
            )
        return carry

    lax.fori_loop(0, (count + UNROLL - 1) // UNROLL, some, 0)
    plan_ref[2 * pairs] = count
    for face in range(face_ref.shape[0]):
        block = face_ref[face]
        plan_ref[2 * pairs + 1 + face] = block
        put_block(faces_ref, face * SIX, pos_ref, dir_ref, block)


def pieces(value):
    high = value.astype(BF16).astype(F32)
    rest = value - high
    mid = rest.astype(BF16).astype(F32)
    return high, mid, rest - mid


def own_terms(rows, sums):
    row = lax.broadcasted_iota(jnp.int32, (8, LANES), 0)
    by_grad = sums[:, :LANES]
    by_curv = sums[:, LANES:]
    first = rows * by_grad[6:7, :] - by_grad
    second = rows * by_curv[6:7, :] - by_curv
    shifted = pltpu.roll(second, 3, 0)
    return first + jnp.where((row >= 3) & (row < 6), shifted, 0.0)


def fold(product):
    return product[0:8] + product[8:16] + product[16:24]


def twice_wide(tall):
    return jnp.concatenate([tall, tall], axis=1)


def remote_operands(rows):
    row = lax.broadcasted_iota(jnp.int32, (8, LANES), 0)
    twice = jnp.where(row == 6, -2.0, -2.0 * rows)
    high, mid, low = pieces(twice)
    products = twice * jnp.where(row < 3, twice, pltpu.roll(twice, 3, 0))
    p_high, p_mid, p_low = pieces(products)
    zero = jnp.zeros_like(low)
    high_mid = jnp.concatenate([high, mid], axis=0).astype(BF16)
    high_low = jnp.concatenate([high, low], axis=0).astype(BF16)
    low_zero = jnp.concatenate([low, zero], axis=0).astype(BF16)
    p_high_mid = jnp.concatenate([p_high, p_mid], axis=0).astype(BF16)
    p_low_zero = jnp.concatenate([p_low, zero], axis=0).astype(BF16)
    distances = jnp.concatenate([high_mid, high_mid, high_low, p_high_mid, p_low_zero], axis=0)
    return distances, jnp.concatenate([high_mid, low_zero], axis=0)


def local_operands(rows):
    row = lax.broadcasted_iota(jnp.int32, (8, LANES), 0)
    square = jnp.sum(rows[0:3] * rows[0:3], axis=0, keepdims=True) + XI
    cross = jnp.sum(rows[0:3] * rows[3:6], axis=0, keepdims=True)
    for_square = jnp.where(row < 3, rows, jnp.where(row == 6, -0.5 * square, 0.0))
    swapped = jnp.where(row < 3, pltpu.roll(rows, 5, 0), pltpu.roll(rows, 3, 0))
    for_cross = jnp.where(row < 6, swapped, jnp.where(row == 6, -cross, 0.0))
    squares = jnp.where(row < 3, 0.25, jnp.zeros_like(rows))
    crosses = jnp.where((row >= 3) & (row < 6), 0.5, jnp.zeros_like(rows))
    halves = []
    for full, own in ((for_square, squares), (for_cross, crosses)):
        high, mid, low = pieces(full)
        tall = [high, high, mid, mid, low, high, own, own, own, jnp.zeros_like(own)]
        tall += [jnp.zeros_like(own)] * 6
        halves.append(jnp.concatenate(tall, axis=0).T)
    return jnp.concatenate(halves, axis=0).astype(BF16)


def local_setup(pos_ref, dir_ref, rows_ref, feature_ref, left_ref, center_ref):
    row = lax.broadcasted_iota(jnp.int32, (8, LANES), 0)
    for block in range(pos_ref.shape[1] // LANES):
        span = slice(block * LANES, (block + 1) * LANES)
        rows = jnp.concatenate(
            [pos_ref[:, span], dir_ref[:, span], jnp.zeros((2, LANES), F32)], axis=0
        )
        center = jnp.mean(rows, axis=1, keepdims=True)
        rows = rows - center
        center_ref[block] = jnp.broadcast_to(center, (8, LANES))
        rows_ref[block] = rows
        feature_ref[block] = local_operands(rows)
        left_ref[block] = twice_wide(remote_operands(rows)[1])


def split(value):
    high = value.astype(BF16)
    return high, (value - high.astype(F32)).astype(BF16)


def pair_coefficients(product):
    squared = jnp.minimum(product[:LANES], 1.0)
    along = product[LANES:]
    log_ratio = jnp.log(squared)
    log_twice = log_ratio + log_ratio
    excess = squared - 1.0
    ratio = excess / squared
    return (
        split(excess * (log_twice + ratio)),
        split((log_twice + ratio * (4.0 - ratio)) * along),
    )


def pair_sums(grad, curv, left, right, remote):
    by_local = jnp.concatenate(
        [jnp.concatenate([grad[k], curv[k]], axis=1) for k in range(2)], axis=0
    )
    by_remote = jnp.concatenate(
        [jnp.concatenate([both[0], both[1]], axis=1) for both in (grad, curv)], axis=0
    )
    for_remote = lax.dot_general(left, by_local, NN, preferred_element_type=F32)
    for_local = lax.dot_general(twice_wide(right), by_remote, NT, preferred_element_type=F32)
    return own_terms(remote, fold(for_remote)), fold(for_local)


def eight_rows(six):
    return jnp.concatenate([six, jnp.zeros((2, LANES), F32)], axis=0)


def cross_kernel(
    local_ref, face_ref, pos_ref, dir_ref, incoming_ref,
    sums_ref, back_ref, rows_ref, feature_ref, left_ref, center_ref,
):
    local_setup(pos_ref, dir_ref, rows_ref, feature_ref, left_ref, center_ref)
    sums_ref[...] = jnp.zeros_like(sums_ref)
    back_ref[...] = jnp.zeros_like(back_ref)

    def some(step, carry):
        pairs = [step * 4 + k for k in range(4)]
        blocks = [local_ref[pair] for pair in pairs]
        rows = [pl.ds(face_ref[pair] * SIX, SIX) for pair in pairs]
        remotes = [
            eight_rows(incoming_ref[row, :]) - center_ref[block] for block, row in zip(blocks, rows)
        ]
        operands = [remote_operands(remote) for remote in remotes]
        products = [
            lax.dot_general(
                feature_ref[block, :, : right.shape[0]], right, NN, preferred_element_type=F32
            )
            for block, (right, _) in zip(blocks, operands)
        ]
        for block, row, remote, (_, right), product in zip(
            blocks, rows, remotes, operands, products
        ):
            grad, curv = pair_coefficients(product)
            remote, local = pair_sums(grad, curv, left_ref[block], right, remote)
            back_ref[row, :] += remote[:SIX]
            sums_ref[block] += local
        return carry

    count = jnp.where(lax.axis_index("body") > 0, local_ref.shape[0] // 4, 0)
    lax.fori_loop(0, count, some, 0)


def main_kernel(
    arrived_ref, sums_in_ref, rows_ref, feature_ref, left_ref, center_ref,
    return_ref, terms_ref,
    sums_ref, list_ref, table_ref, sem,
    dist_a, dist_b, right_a, right_b, remote_a, remote_b,
):
    peers = arrived_ref.shape[0] // MSG
    slots = 2 * peers
    num_blocks = terms_ref.shape[0]
    marks = arrived_ref[pl.ds(RET, peers, stride=MSG), :].astype(BF16)
    pick = (
        lax.broadcasted_iota(jnp.int32, (16, LANES), 0)
        == lax.broadcasted_iota(jnp.int32, (16, LANES), 1)
    ).astype(BF16)
    found = lax.dot_general(pick, marks, NT, preferred_element_type=F32)
    wide = jnp.concatenate([found[0:1], found[1:2]], axis=1)
    valid = wide >= 0.0
    slot = lax.broadcasted_iota(jnp.int32, (1, slots), 1)
    one = lax.broadcasted_iota(jnp.int32, (slots, slots), 0)
    before = (one < lax.broadcasted_iota(jnp.int32, (slots, slots), 1)).astype(BF16)
    ones = jnp.broadcast_to(valid.astype(F32), (16, slots)).astype(BF16)
    place = lax.dot_general(ones, before, NN, preferred_element_type=F32)[0:1]
    hot = (one.astype(F32) == place) & valid
    row = lax.broadcasted_iota(jnp.int32, (16, slots), 0)
    second = slot >= peers
    peer = jnp.where(second, slot - peers, slot).astype(F32)
    codes = jnp.where(row == 0, jnp.broadcast_to(wide, (16, slots)), 0.0)
    codes = jnp.where(row == 1, jnp.broadcast_to(peer, (16, slots)), codes)
    codes = jnp.where(row == 2, jnp.broadcast_to(second.astype(F32), (16, slots)), codes)
    ordered = lax.dot_general(
        codes.astype(BF16), hot.astype(F32).astype(BF16), NT, preferred_element_type=F32
    )
    ordered = ordered[:8].astype(jnp.int32)
    total = jnp.sum(valid.astype(F32), axis=1, keepdims=True).astype(jnp.int32)
    row = row[:8]
    base = ordered[1:2]
    shift = ordered[2:3] * SIX
    table = jnp.where(row == 0, ordered[0:1], 0)
    table = jnp.where(row == 1, base * MSG + shift, table)
    table = jnp.where(row == 2, base * RET + shift, table)
    list_ref[:, :slots] = jnp.where(row == 3, total, table)
    copy = pltpu.make_async_copy(list_ref, table_ref, sem)
    copy.start()
    sums_ref[0:num_blocks] = sums_in_ref[...]
    sums_ref[num_blocks] = jnp.zeros((8, 2 * LANES), F32)
    copy.wait()
    count = table_ref[3, 0]

    def listed(group, k):
        return jnp.clip(group * GROUP + k, 0, count - 1)

    def distances(group, dist_ref, right_ref, remote_ref):
        for k in range(GROUP):
            pair = listed(group, k)
            block = table_ref[0, pair]
            rows = eight_rows(arrived_ref[pl.ds(table_ref[1, pair], SIX), :]) - center_ref[block]
            right, sums_right = remote_operands(rows)
            remote_ref[k] = rows
            right_ref[k] = sums_right
            dist_ref[k] = lax.dot_general(
                feature_ref[block, :, : right.shape[0]], right, NN, preferred_element_type=F32
            )

    def sums(group, dist_ref, right_ref, remote_ref):
        for k in range(GROUP):
            pair = group * GROUP + k
            known = listed(group, k)
            block = table_ref[0, known]
            target = jnp.where(pair < count, block, num_blocks)
            grad, curv = pair_coefficients(dist_ref[k])
            remote, local = pair_sums(grad, curv, left_ref[block], right_ref[k], remote_ref[k])
            return_ref[pl.ds(table_ref[2, known], SIX), :] = remote[:SIX]
            sums_ref[target] += local

    def two_groups(step, carry):
        group = 2 * step
        distances(group + 1, dist_b, right_b, remote_b)
        sums(group, dist_a, right_a, remote_a)
        distances(group + 2, dist_a, right_a, remote_a)
        sums(group + 1, dist_b, right_b, remote_b)
        return carry

    @pl.when(count > 0)
    def _():
        distances(0, dist_a, right_a, remote_a)
        lax.fori_loop(0, (count + 2 * GROUP - 1) // (2 * GROUP), two_groups, 0)

    for block in range(num_blocks):
        terms_ref[block] = own_terms(rows_ref[block], sums_ref[block])


def finish_kernel(
    plan_ref, returned_ref, terms_ref, back_ref,
    grad_ref, hess_ref,
    total_ref,
):
    num_blocks = terms_ref.shape[0]
    faces = back_ref.shape[0] // SIX
    pairs = (plan_ref.shape[0] - 1 - faces) // 2
    total_ref[0:num_blocks] = terms_ref[...]
    for face in range(faces):
        block = plan_ref[2 * pairs + 1 + face]
        total_ref[block, 0:SIX, :] += back_ref[face * SIX : face * SIX + SIX, :]
    count = plan_ref[2 * pairs]

    def some(step, carry):
        for k in range(UNROLL):
            pair = step * UNROLL + k
            block = jnp.where(pair < count, plan_ref[pairs + pair], num_blocks)
            total_ref[block, 0:SIX, :] += returned_ref[pl.ds(plan_ref[pair], SIX), :]
        return carry

    lax.fori_loop(0, (count + UNROLL - 1) // UNROLL, some, 0)
    for block in range(num_blocks):
        span = slice(block * LANES, (block + 1) * LANES)
        grad_ref[:, span] = SCALE * total_ref[block, 0:3, :]
        hess_ref[:, span] = SCALE * total_ref[block, 3:6, :]


def smem():
    return pl.BlockSpec(memory_space=pltpu.SMEM)


def vmem():
    return pl.BlockSpec(memory_space=pltpu.VMEM)


def on_chip(*shape, dtype=F32):
    return pltpu.VMEM(shape, dtype)


def held(*values):
    return [pltpu.with_memory_space_constraint(value, pltpu.VMEM) for value in values]


def exchange(rows, peers):
    count = rows.shape[0] // peers
    return lax.all_to_all(
        rows.reshape(peers, count, 1, LANES), "blk", split_axis=0, concat_axis=0, tiled=True
    ).reshape(rows.shape)


def per_device(
    positions, direction, pair_local, pair_peer, pair_shift, pair_count,
    face_index, cross_local, cross_face,
):
    num_blocks = positions.shape[1] // LANES
    peers = lax.axis_size("blk")
    faces = face_index.shape[0]
    setup = (
        on_chip(num_blocks, 8, LANES),
        on_chip(num_blocks, 2 * LANES, LANES, dtype=BF16),
        on_chip(num_blocks, 32, 2 * LANES, dtype=BF16),
        on_chip(num_blocks, 8, LANES),
    )
    send, face_rows, plan = pl.pallas_call(
        pack_kernel,
        name="pack",
        out_shape=(
            on_chip(peers * MSG, LANES),
            on_chip(faces * SIX, LANES),
            pltpu.SMEM((2 * pair_local.shape[0] + 1 + faces,), jnp.int32),
        ),
        in_specs=[smem()] * 5 + [vmem()] * 2,
        out_specs=(vmem(), vmem(), smem()),
        scratch_shapes=[pltpu.SMEM((peers,), jnp.int32)],
    )(pair_local, pair_peer, pair_shift, pair_count, face_index, positions, direction)
    arrived = exchange(send, peers)
    incoming = from_behind(face_rows, "body", 1)
    sums, back, *local = pl.pallas_call(
        cross_kernel,
        name="cross",
        out_shape=(on_chip(num_blocks, 8, 2 * LANES), on_chip(faces * SIX, LANES)) + setup,
        in_specs=[smem()] * 2 + [vmem()] * 3,
        out_specs=(vmem(),) * 6,
    )(cross_local, cross_face, positions, direction, *held(incoming))
    face_back = from_behind(back, "body", -1)
    outgoing, terms = pl.pallas_call(
        main_kernel,
        name="pairs",
        out_shape=(on_chip(peers * RET, LANES), on_chip(num_blocks, 8, LANES)),
        in_specs=[vmem()] * 6,
        out_specs=(vmem(), vmem()),
        scratch_shapes=[
            pltpu.VMEM((num_blocks + 1, 8, 2 * LANES), F32),
            pltpu.VMEM((8, LANES), jnp.int32),
            pltpu.SMEM((8, LANES), jnp.int32),
            pltpu.SemaphoreType.DMA,
        ]
        + [pltpu.VMEM((GROUP, 2 * LANES, LANES), F32)] * 2
        + [pltpu.VMEM((GROUP, 32, LANES), BF16)] * 2
        + [pltpu.VMEM((GROUP, 8, LANES), F32)] * 2,
    )(*held(arrived, sums, *local))
    returned = exchange(outgoing, peers)
    return pl.pallas_call(
        finish_kernel,
        name="finish",
        out_shape=[jax.ShapeDtypeStruct((3, num_blocks * LANES), F32)] * 2,
        in_specs=[smem()] + [vmem()] * 3,
        out_specs=(vmem(), vmem()),
        scratch_shapes=[pltpu.VMEM((num_blocks + 1, 8, LANES), F32)],
    )(plan, *held(returned, terms, face_back))


def solution(mesh):
    split_all = P(("blk", "body"))
    wide = P(None, ("blk", "body"))
    return jax.shard_map(
        per_device,
        mesh=mesh,
        in_specs=(wide, wide) + (split_all,) * 7,
        out_specs=(wide, wide),
        check_vma=False,
    )
```

time: 62.7 us -> 60.4 us (0.963); the launches traced: 63.1 us -> 60 us
  starting transfers between devices: 26 us -> 23.7 us
  local copies, waits for them, and re-layouts: 0 us -> 2.19 us
  Pallas kernels: 12.4 us -> 10.5 us
  waiting for transfers between devices: 23.3 us -> 22.3 us
    all_to_all x2, waiting for transfers between devices: 19.1 us -> 16.7 us  [exchange(): lax.all_to_all(rows.reshape(peers, count, 1, LANES), 'blk', split_axis=0,...]
    all_to_all x2, starting transfers between devices: 20.8 us -> 18.4 us  [exchange(): lax.all_to_all(rows.reshape(peers, count, 1, LANES), 'blk', split_axis=0,...]
    unnamed x0 -> x4, local copies, waits for them, and re-layouts: none -> 2.19 us
    ppermute x2, waiting for transfers between devices: 4.25 us -> 5.57 us  [from_behind(): lax.ppermute(value, axis, [(source, source + steps) for source in range(f...]
    pallas_call x1, Pallas kernels: 7.59 us -> 6.43 us  [per_device(): pl.pallas_call(main_kernel, name='pairs', out_shape=(on_chip(peers * RET,...]
    pallas_call x1, Pallas kernels: 1.56 us -> 0.82 us  [per_device(): pl.pallas_call(finish_kernel, name='finish', out_shape=[jax.ShapeDtypeStr...]
where the time goes in v1:
time: 60.4 us; the launch traced here: 60 us
  starting transfers between devices  23.7 us (39%)
  waiting for transfers between devices  22.3 us (37%)
  Pallas kernels  10.5 us (17%)
  local copies, waits for them, and re-layouts  2.19 us (4%)
  between operations  1.33 us (2%)
    all_to_all x2, starting transfers between devices, exchange(): lax.all_to_all(rows.reshape(peers, count, 1, LANES), 'blk', split_axis=0,...  18.4 us
    all_to_all x2, waiting for transfers between devices, exchange(): lax.all_to_all(rows.reshape(peers, count, 1, LANES), 'blk', split_axis=0,...  16.7 us
    pallas_call x1, Pallas kernels, per_device(): pl.pallas_call(main_kernel, name='pairs', out_shape=(on_chip(peers * RET,...  6.43 us
    ppermute x2, waiting for transfers between devices, from_behind(): lax.ppermute(value, axis, [(source, source + steps) for source in range(f...  5.57 us
    ppermute x2, starting transfers between devices, from_behind(): lax.ppermute(value, axis, [(source, source + steps) for source in range(f...  5.29 us
    unnamed x4, local copies, waits for them, and re-layouts  2.19 us
    pallas_call x1, Pallas kernels, per_device(): pl.pallas_call(pack_kernel, name='pack', out_shape=(on_chip(peers * MSG,...  1.98 us
    pallas_call x1, Pallas kernels, per_device(): pl.pallas_call(cross_kernel, name='cross', out_shape=(on_chip(num_blocks,...  1.25 us
  transfers between devices with their start and end apart: 4, of which 4 were waited for; matrix products, arithmetic and copies ran while one was open for 0% of the time, Pallas kernels for 2%

profile of v1, /device:TPU:1, one launch (start us, length us, event | category | flops | bytes accessed | tf_op | source)
XLA Modules:
  0.0 60.0 jit_solution(11389593423753638013)
XLA Ops:
  1.3 2.0 %pack.1 = (f32[832,128]{1,0:T(8,128)}, f32[24,128]{1,0:T(8,128)S(1)}, s32[133]{0:T(256)S(4)}) custom-call(s32[64]{0:T(128)} %local_ref.2, s32[64]{0:T(128)} %peer_ref.1, s32[64]{0:T(128)} %shift_ref.1, s32[1]{0:T(128)S(6)} %copy.13.count_ref, s32[4]{0:T(128)} %face_ref.2, f32[3,2048]{1,0:T(4,128)} %pos_ref.3, f32[3,2048]{1,0:T(4,128)} %dir_ref.3), custom_call_target="tpu_custom_call" | custom-call | tf_op jit(solution)/shard_map/pack/pallas_call | solution.py:374
  3.3 11.6 %all-to-all-start = ((f32[64,13,1,128]{3,2,1,0:T(1,128)}), f32[64,13,1,128]{3,2,1,0:T(1,128)S(1)}, u32[]{:S(2)}, u32[]{:S(2)}) async-start(f32[64,13,1,128]{3,2,1,0:T(1,128)} %bitcast), calls=%async_computation | async-start | bytes 851968 | tf_op jit(solution)/shard_map/all_to_all | solution.py:356
  14.9 4.0 %collective-permute-start = (f32[24,128]{1,0:T(8,128)S(1)}, f32[24,128]{1,0:T(8,128)S(1)}, u32[]{:S(2)}, u32[]{:S(2)}) collective-permute-start(f32[24,128]{1,0:T(8,128)S(1)} %get-tuple-element.15), channel_id=1, source_target_pairs={{0,1},{1,2},{2,3},{3,4},{4,5},{5,6},{6,7},{8,9},{9,10},{10,11},{11... | collective-permute-start | bytes 36872 | tf_op jit(solution)/shard_map/ppermute | solution.py:25
  18.9 0.8 %collective-permute-done.incoming_ref = f32[24,128]{1,0:T(8,128)S(1)} collective-permute-done((f32[24,128]{1,0:T(8,128)S(1)}, f32[24,128]{1,0:T(8,128)S(1)}, u32[]{:S(2)}, u32[]{:S(2)}) %collective-permute-start) | collective-permute-done | bytes 12320 | tf_op jit(solution)/shard_map/ppermute | solution.py:25
  19.7 1.3 %cross.1 = (f32[16,8,256]{2,1,0:T(8,128)S(1)}, f32[24,128]{1,0:T(8,128)S(1)}, f32[16,8,128]{2,1,0:T(8,128)S(1)}, bf16[16,256,128]{2,1,0:T(8,128)(2,1)S(1)}, bf16...) custom-call(s32[8]{0:T(128)} %local_ref.3, s32[8]{0:T(128)} %face_ref.3, f32[3,2048]{1,0:T(4,128)} %pos_ref.3, ...), custom_call_target="tpu_custom_call" | custom-call | tf_op jit(solution)/shard_map/cross/pallas_call | solution.py:388
  20.9 0.0 copy-start
  21.0 1.0 %copy-done = bf16[16,256,128]{2,1,0:T(8,128)(2,1)} copy-done((bf16[16,256,128]{2,1,0:T(8,128)(2,1)}, bf16[16,256,128]{2,1,0:T(8,128)(2,1)S(1)}, u32[]{:S(2)}) %copy-start) | copy-done | bytes 1048600
  21.9 8.2 %all-to-all-done = f32[64,13,1,128]{3,2,1,0:T(1,128)S(1)} async-done(((f32[64,13,1,128]{3,2,1,0:T(1,128)}), f32[64,13,1,128]{3,2,1,0:T(1,128)S(1)}, u32[]{:S(2)}, u32[]{:S(2)}) %all-to-all-start) | async-done | bytes 426016 | tf_op jit(solution)/shard_map/all_to_all | solution.py:356
  30.1 0.0 copy-start.1
  30.1 1.2 %copy-done.1 = bf16[16,256,128]{2,1,0:T(8,128)(2,1)S(1)} copy-done((bf16[16,256,128]{2,1,0:T(8,128)(2,1)S(1)}, bf16[16,256,128]{2,1,0:T(8,128)(2,1)}, u32[]{:S(2)}) %copy-start.1) | copy-done | bytes 1048600
  31.4 6.4 %pairs.1 = (f32[768,128]{1,0:T(8,128)}, f32[16,8,128]{2,1,0:T(8,128)S(1)}) custom-call(f32[832,128]{1,0:T(8,128)S(1)} %bitcast.4, f32[16,8,256]{2,1,0:T(8,128)S(1)} %get-tuple-element.16.sums_in_ref, f32[16,8,128]{2,1,0:T(8,128)S(1)} %get-tuple-element.17.rows_ref, bf16[16,256,128]{2,1,0:T(8,128)(2,1)S(1)} %copy-done.1, ...), custom_call_target="tpu_custom_call" | custom-call | tf_op jit(solution)/shard_map/pairs/pallas_call | solution.py:396
  37.8 6.8 %all-to-all-start.1 = ((f32[64,12,1,128]{3,2,1,0:T(1,128)}), f32[64,12,1,128]{3,2,1,0:T(1,128)S(1)}, u32[]{:S(2)}, u32[]{:S(2)}) async-start(f32[64,12,1,128]{3,2,1,0:T(1,128)} %bitcast.2), calls=%async_computation.1 | async-start | bytes 786432 | tf_op jit(solution)/shard_map/all_to_all | solution.py:356
  44.6 1.3 %collective-permute-start.1 = (f32[24,128]{1,0:T(8,128)S(1)}, f32[24,128]{1,0:T(8,128)S(1)}, u32[]{:S(2)}, u32[]{:S(2)}) collective-permute-start(f32[24,128]{1,0:T(8,128)S(1)} %get-tuple-element.23), channel_id=1, source_target_pairs={{1,0},{2,1},{3,2},{4,3},{5,4},{6,5},{7,6},{9,8},{10,9},{11,10},{12... | collective-permute-start | bytes 36872 | tf_op jit(solution)/shard_map/ppermute | solution.py:25
  45.9 4.8 %collective-permute-done.1.back_ref = f32[24,128]{1,0:T(8,128)S(1)} collective-permute-done((f32[24,128]{1,0:T(8,128)S(1)}, f32[24,128]{1,0:T(8,128)S(1)}, u32[]{:S(2)}, u32[]{:S(2)}) %collective-permute-start.1) | collective-permute-done | bytes 12320 | tf_op jit(solution)/shard_map/ppermute | solution.py:25
  50.7 8.5 %all-to-all-done.1 = f32[64,12,1,128]{3,2,1,0:T(1,128)S(1)} async-done(((f32[64,12,1,128]{3,2,1,0:T(1,128)}), f32[64,12,1,128]{3,2,1,0:T(1,128)S(1)}, u32[]{:S(2)}, u32[]{:S(2)}) %all-to-all-start.1) | async-done | bytes 393248 | tf_op jit(solution)/shard_map/all_to_all | solution.py:356
  59.1 0.8 %finish.1 = (f32[3,2048]{1,0:T(4,128)}, f32[3,2048]{1,0:T(4,128)}) custom-call(s32[133]{0:T(256)S(4)} %get-tuple-element.13.plan_ref, f32[768,128]{1,0:T(8,128)S(1)} %bitcast.5, f32[16,8,128]{2,1,0:T(8,128)S(1)} %get-tuple-element.22.terms_ref, f32[24,128]{1,0:T(8,128)S(1)} %collective-permute-done.1.back_ref), custom_call_target="tpu_custom_call" | custom-call | tf_op jit(solution)/shard_map/finish/pallas_call | solution.py:413
Async XLA Ops:
  3.3 26.9 %all-to-all-start = ((f32[64,13,1,128]{3,2,1,0:T(1,128)}), f32[64,13,1,128]{3,2,1,0:T(1,128)S(1)}, u32[]{:S(2)}, u32[]{:S(2)}) async-start(f32[64,13,1,128]{3,2,1,0:T(1,128)} %bitcast), calls=%async_computation | async-start | bytes 851968 | tf_op jit(solution)/shard_map/all_to_all | solution.py:356
  14.9 4.8 %collective-permute-start = (f32[24,128]{1,0:T(8,128)S(1)}, f32[24,128]{1,0:T(8,128)S(1)}, u32[]{:S(2)}, u32[]{:S(2)}) collective-permute-start(f32[24,128]{1,0:T(8,128)S(1)} %get-tuple-element.15), channel_id=1, source_target_pairs={{0,1},{1,2},{2,3},{3,4},{4,5},{5,6},{6,7},{8,9},{9,10},{10,11},{11... | collective-permute-start | bytes 36872 | tf_op jit(solution)/shard_map/ppermute | solution.py:25
  20.9 1.0 %copy-start = (bf16[16,256,128]{2,1,0:T(8,128)(2,1)}, bf16[16,256,128]{2,1,0:T(8,128)(2,1)S(1)}, u32[]{:S(2)}) copy-start(bf16[16,256,128]{2,1,0:T(8,128)(2,1)S(1)} %get-tuple-element.18.feature_ref) | copy-start | bytes 3145732
  30.1 1.2 %copy-start.1 = (bf16[16,256,128]{2,1,0:T(8,128)(2,1)S(1)}, bf16[16,256,128]{2,1,0:T(8,128)(2,1)}, u32[]{:S(2)}) copy-start(bf16[16,256,128]{2,1,0:T(8,128)(2,1)} %copy-done) | copy-start | bytes 3145732
  37.8 21.3 %all-to-all-start.1 = ((f32[64,12,1,128]{3,2,1,0:T(1,128)}), f32[64,12,1,128]{3,2,1,0:T(1,128)S(1)}, u32[]{:S(2)}, u32[]{:S(2)}) async-start(f32[64,12,1,128]{3,2,1,0:T(1,128)} %bitcast.2), calls=%async_computation.1 | async-start | bytes 786432 | tf_op jit(solution)/shard_map/all_to_all | solution.py:356
  44.6 6.1 %collective-permute-start.1 = (f32[24,128]{1,0:T(8,128)S(1)}, f32[24,128]{1,0:T(8,128)S(1)}, u32[]{:S(2)}, u32[]{:S(2)}) collective-permute-start(f32[24,128]{1,0:T(8,128)S(1)} %get-tuple-element.23), channel_id=1, source_target_pairs={{1,0},{2,1},{3,2},{4,3},{5,4},{6,5},{7,6},{9,8},{10,9},{11,10},{12... | collective-permute-start | bytes 36872 | tf_op jit(solution)/shard_map/ppermute | solution.py:25

commit v2 on v1

--- a/solution.py
+++ b/solution.py
@@ -1,3 +1,5 @@
+import functools
+
 import jax
 import jax.numpy as jnp
 from jax import lax
@@ -6,12 +8,14 @@
 from jax.sharding import PartitionSpec as P
 
 XI = 0.1
+TWICE_LN2 = 1.3862943611198906
 SCALE = 0.02
 LANES = 128
 SIX = 6
 MSG = 13
 RET = 12
 GROUP = 3
+IN_TURN = 3
 UNROLL = 4
 F32 = jnp.float32
 BF16 = jnp.bfloat16
@@ -144,7 +148,7 @@
         center_ref[block] = jnp.broadcast_to(center, (8, LANES))
         rows_ref[block] = rows
         feature_ref[block] = local_operands(rows)
-        left_ref[block] = twice_wide(remote_operands(rows)[1])
+        left_ref[block] = remote_operands(rows)[1]
 
 
 def split(value):
@@ -155,8 +159,7 @@
 def pair_coefficients(product):
     squared = jnp.minimum(product[:LANES], 1.0)
     along = product[LANES:]
-    log_ratio = jnp.log(squared)
-    log_twice = log_ratio + log_ratio
+    log_twice = TWICE_LN2 * lax.log2(squared)
     excess = squared - 1.0
     ratio = excess / squared
     return (
@@ -170,10 +173,10 @@
         [jnp.concatenate([grad[k], curv[k]], axis=1) for k in range(2)], axis=0
     )
     by_remote = jnp.concatenate(
-        [jnp.concatenate([both[0], both[1]], axis=1) for both in (grad, curv)], axis=0
-    )
-    for_remote = lax.dot_general(left, by_local, NN, preferred_element_type=F32)
-    for_local = lax.dot_general(twice_wide(right), by_remote, NT, preferred_element_type=F32)
+        [jnp.concatenate([grad[k].T, curv[k].T], axis=1) for k in range(2)], axis=0
+    )
+    for_remote = lax.dot_general(twice_wide(left), by_local, NN, preferred_element_type=F32)
+    for_local = lax.dot_general(twice_wide(right), by_remote, NN, preferred_element_type=F32)
     return own_terms(remote, fold(for_remote)), fold(for_local)
 
 
@@ -217,10 +220,10 @@
 
 
 def main_kernel(
-    arrived_ref, sums_in_ref, rows_ref, feature_ref, left_ref, center_ref,
+    plan_ref, arrived_ref, back_ref, sums_in_ref, rows_ref, feature_ref, left_ref, center_ref,
     return_ref, terms_ref,
     sums_ref, list_ref, table_ref, sem,
-    dist_a, dist_b, right_a, right_b, remote_a, remote_b,
+    *buffers,
 ):
     peers = arrived_ref.shape[0] // MSG
     slots = 2 * peers
@@ -290,35 +293,40 @@
             return_ref[pl.ds(table_ref[2, known], SIX), :] = remote[:SIX]
             sums_ref[target] += local
 
-    def two_groups(step, carry):
-        group = 2 * step
-        distances(group + 1, dist_b, right_b, remote_b)
-        sums(group, dist_a, right_a, remote_a)
-        distances(group + 2, dist_a, right_a, remote_a)
-        sums(group + 1, dist_b, right_b, remote_b)
+    sets = [buffers[k::IN_TURN] for k in range(IN_TURN)]
+
+    def some_groups(step, carry):
+        group = IN_TURN * step
+        for k in range(1, IN_TURN):
+            distances(group + k, *sets[k])
+            sums(group + k - 1, *sets[k - 1])
+        distances(group + IN_TURN, *sets[0])
+        sums(group + IN_TURN - 1, *sets[-1])
         return carry
 
     @pl.when(count > 0)
     def _():
-        distances(0, dist_a, right_a, remote_a)
-        lax.fori_loop(0, (count + 2 * GROUP - 1) // (2 * GROUP), two_groups, 0)
+        distances(0, *sets[0])
+        lax.fori_loop(
+            0, (count + IN_TURN * GROUP - 1) // (IN_TURN * GROUP), some_groups, 0
+        )
 
     for block in range(num_blocks):
         terms_ref[block] = own_terms(rows_ref[block], sums_ref[block])
+    faces = back_ref.shape[0] // SIX
+    for face in range(faces):
+        block = plan_ref[plan_ref.shape[0] - faces + face]
+        terms_ref[block, 0:SIX, :] += back_ref[face * SIX : face * SIX + SIX, :]
 
 
 def finish_kernel(
-    plan_ref, returned_ref, terms_ref, back_ref,
+    num_pairs, plan_ref, returned_ref, terms_ref,
     grad_ref, hess_ref,
     total_ref,
 ):
     num_blocks = terms_ref.shape[0]
-    faces = back_ref.shape[0] // SIX
-    pairs = (plan_ref.shape[0] - 1 - faces) // 2
+    pairs = num_pairs
     total_ref[0:num_blocks] = terms_ref[...]
-    for face in range(faces):
-        block = plan_ref[2 * pairs + 1 + face]
-        total_ref[block, 0:SIX, :] += back_ref[face * SIX : face * SIX + SIX, :]
     count = plan_ref[2 * pairs]
 
     def some(step, carry):
@@ -341,6 +349,10 @@
 
 def vmem():
     return pl.BlockSpec(memory_space=pltpu.VMEM)
+
+
+def limit(mib):
+    return pltpu.CompilerParams(vmem_limit_bytes=mib << 20)
 
 
 def on_chip(*shape, dtype=F32):
@@ -368,7 +380,7 @@
     setup = (
         on_chip(num_blocks, 8, LANES),
         on_chip(num_blocks, 2 * LANES, LANES, dtype=BF16),
-        on_chip(num_blocks, 32, 2 * LANES, dtype=BF16),
+        on_chip(num_blocks, 32, LANES, dtype=BF16),
         on_chip(num_blocks, 8, LANES),
     )
     send, face_rows, plan = pl.pallas_call(
@@ -388,6 +400,7 @@
     sums, back, *local = pl.pallas_call(
         cross_kernel,
         name="cross",
+        compiler_params=limit(8),
         out_shape=(on_chip(num_blocks, 8, 2 * LANES), on_chip(faces * SIX, LANES)) + setup,
         in_specs=[smem()] * 2 + [vmem()] * 3,
         out_specs=(vmem(),) * 6,
@@ -396,8 +409,9 @@
     outgoing, terms = pl.pallas_call(
         main_kernel,
         name="pairs",
+        compiler_params=limit(8),
         out_shape=(on_chip(peers * RET, LANES), on_chip(num_blocks, 8, LANES)),
-        in_specs=[vmem()] * 6,
+        in_specs=[smem()] + [vmem()] * 7,
         out_specs=(vmem(), vmem()),
         scratch_shapes=[
             pltpu.VMEM((num_blocks + 1, 8, 2 * LANES), F32),
@@ -405,19 +419,19 @@
             pltpu.SMEM((8, LANES), jnp.int32),
             pltpu.SemaphoreType.DMA,
         ]
-        + [pltpu.VMEM((GROUP, 2 * LANES, LANES), F32)] * 2
-        + [pltpu.VMEM((GROUP, 32, LANES), BF16)] * 2
-        + [pltpu.VMEM((GROUP, 8, LANES), F32)] * 2,
-    )(*held(arrived, sums, *local))
+        + [pltpu.VMEM((GROUP, 2 * LANES, LANES), F32)] * IN_TURN
+        + [pltpu.VMEM((GROUP, 32, LANES), BF16)] * IN_TURN
+        + [pltpu.VMEM((GROUP, 8, LANES), F32)] * IN_TURN,
+    )(plan, *held(arrived, face_back, sums, *local))
     returned = exchange(outgoing, peers)
     return pl.pallas_call(
-        finish_kernel,
+        functools.partial(finish_kernel, pair_local.shape[0]),
         name="finish",
         out_shape=[jax.ShapeDtypeStruct((3, num_blocks * LANES), F32)] * 2,
-        in_specs=[smem()] + [vmem()] * 3,
+        in_specs=[smem()] + [vmem()] * 2,
         out_specs=(vmem(), vmem()),
         scratch_shapes=[pltpu.VMEM((num_blocks + 1, 8, LANES), F32)],
-    )(plan, *held(returned, terms, face_back))
+    )(plan, *held(returned, terms))
 
 
 def solution(mesh):

time: 60.4 us -> 61.1 us (1.012)
  the two profiles are of different devices: /device:TPU:1 before, /device:TPU:199 now
where the time goes in v2:
time: 61.1 us; the launch traced here: 61 us
  blocking collectives  26.6 us (44%)
  starting transfers between devices  18.2 us (30%)
  Pallas kernels  8.94 us (15%)
  waiting for transfers between devices  5.84 us (10%)
  between operations  1.33 us (2%)
    all_to_all x1, blocking collectives, exchange(): lax.all_to_all(rows.reshape(peers, count, 1, LANES), 'blk', split_axis=0,...  26.6 us
    all_to_all x1, starting transfers between devices, exchange(): lax.all_to_all(rows.reshape(peers, count, 1, LANES), 'blk', split_axis=0,...  11.1 us
    ppermute x2, starting transfers between devices, from_behind(): lax.ppermute(value, axis, [(source, source + steps) for source in range(f...  7.13 us
    ppermute x2, waiting for transfers between devices, from_behind(): lax.ppermute(value, axis, [(source, source + steps) for source in range(f...  5.39 us
    pallas_call x1, Pallas kernels, per_device(): pl.pallas_call(main_kernel, name='pairs', compiler_params=limit(8), out_s...  3.98 us
    pallas_call x1, Pallas kernels, per_device(): pl.pallas_call(pack_kernel, name='pack', out_shape=(on_chip(peers * MSG,...  2.07 us
    pallas_call x1, Pallas kernels, per_device(): pl.pallas_call(cross_kernel, name='cross', compiler_params=limit(8), out_...  2.04 us
  transfers between devices with their start and end apart: 3, of which 3 were waited for; matrix products, arithmetic and copies ran while one was open for 0% of the time, Pallas kernels for 3%

profile of v2, /device:TPU:199, one launch (start us, length us, event | category | flops | bytes accessed | tf_op | source)
XLA Modules:
  0.0 61.0 jit_solution(16409863168500149104)
XLA Ops:
  1.3 2.1 %pack.1 = (f32[832,128]{1,0:T(8,128)}, f32[24,128]{1,0:T(8,128)S(1)}, s32[133]{0:T(256)S(4)}) custom-call(s32[64]{0:T(128)} %local_ref.2, s32[64]{0:T(128)} %peer_ref.1, s32[64]{0:T(128)} %shift_ref.1, s32[1]{0:T(128)S(6)} %copy.13.count_ref, s32[4]{0:T(128)} %face_ref.2, f32[3,2048]{1,0:T(4,128)} %pos_ref.3, f32[3,2048]{1,0:T(4,128)} %dir_ref.3), custom_call_target="tpu_custom_call" | custom-call | tf_op jit(solution)/shard_map/pack/pallas_call | solution.py:386
  3.3 0.0 copy-start
  3.3 0.0 copy-start.1
  3.3 11.1 %all-to-all-start = ((f32[64,13,1,128]{3,2,1,0:T(1,128)}), f32[64,13,1,128]{3,2,1,0:T(1,128)S(1)}, u32[]{:S(2)}, u32[]{:S(2)}) async-start(f32[64,13,1,128]{3,2,1,0:T(1,128)} %bitcast), calls=%async_computation | async-start | bytes 851968 | tf_op jit(solution)/shard_map/all_to_all | solution.py:368
  14.5 0.0 copy-start.2
  14.5 0.0 copy-start.3
  14.5 5.2 %collective-permute-start = (f32[24,128]{1,0:T(8,128)S(1)}, f32[24,128]{1,0:T(8,128)S(1)}, u32[]{:S(2)}, u32[]{:S(2)}) collective-permute-start(f32[24,128]{1,0:T(8,128)S(1)} %get-tuple-element.15), channel_id=1, source_target_pairs={{0,1},{1,2},{2,3},{3,4},{4,5},{5,6},{6,7},{8,9},{9,10},{10,11},{11... | collective-permute-start | bytes 36872 | tf_op jit(solution)/shard_map/ppermute | solution.py:29
  19.7 0.8 %collective-permute-done.incoming_ref = f32[24,128]{1,0:T(8,128)S(1)} collective-permute-done((f32[24,128]{1,0:T(8,128)S(1)}, f32[24,128]{1,0:T(8,128)S(1)}, u32[]{:S(2)}, u32[]{:S(2)}) %collective-permute-start) | collective-permute-done | bytes 12320 | tf_op jit(solution)/shard_map/ppermute | solution.py:29
  20.5 0.0 copy-done
  20.5 0.0 copy-done.1
  20.5 0.0 copy-done.2
  20.5 0.0 copy-done.3
  20.5 2.0 %cross.1 = (f32[16,8,256]{2,1,0:T(8,128)S(1)}, f32[24,128]{1,0:T(8,128)S(1)}, f32[16,8,128]{2,1,0:T(8,128)S(1)}, bf16[16,256,128]{2,1,0:T(8,128)(2,1)S(1)}, bf16...) custom-call(s32[8]{0:T(128)S(1)} %copy-done.2, s32[8]{0:T(128)S(1)} %copy-done.3, f32[3,2048]{1,0:T(4,128)S(1)} %copy-done, ...), custom_call_target="tpu_custom_call" | custom-call | tf_op jit(solution)/shard_map/cross/pallas_call | solution.py:400
  22.6 1.9 %collective-permute-start.1 = (f32[24,128]{1,0:T(8,128)S(1)}, f32[24,128]{1,0:T(8,128)S(1)}, u32[]{:S(2)}, u32[]{:S(2)}) collective-permute-start(f32[24,128]{1,0:T(8,128)S(1)} %get-tuple-element.16), channel_id=1, source_target_pairs={{1,0},{2,1},{3,2},{4,3},{5,4},{6,5},{7,6},{9,8},{10,9},{11,10},{12... | collective-permute-start | bytes 36872 | tf_op jit(solution)/shard_map/ppermute | solution.py:29
  24.5 4.6 %collective-permute-done.1.back_ref = f32[24,128]{1,0:T(8,128)S(1)} collective-permute-done((f32[24,128]{1,0:T(8,128)S(1)}, f32[24,128]{1,0:T(8,128)S(1)}, u32[]{:S(2)}, u32[]{:S(2)}) %collective-permute-start.1) | collective-permute-done | bytes 12320 | tf_op jit(solution)/shard_map/ppermute | solution.py:29
  29.1 0.5 all-to-all-done
  29.5 4.0 %pairs.1 = (f32[768,128]{1,0:T(8,128)S(1)}, f32[16,8,128]{2,1,0:T(8,128)S(1)}) custom-call(s32[133]{0:T(256)S(4)} %get-tuple-element.13.plan_ref, f32[832,128]{1,0:T(8,128)S(1)} %bitcast.4, f32[24,128]{1,0:T(8,128)S(1)} %collective-permute-done.1.back_ref, f32[16,8,256]{2,1,0:T(8,128)S(1)} %get-tuple-element.17.sums_in_ref, ...), custom_call_target="tpu_custom_call" | custom-call | tf_op jit(solution)/shard_map/pairs/pallas_call | solution.py:409
  33.5 26.6 %all_to_all.10 = f32[64,12,1,128]{3,2,1,0:T(1,128)S(1)} all-to-all(f32[64,12,1,128]{3,2,1,0:T(1,128)S(1)} %bitcast.6), channel_id=1, replica_groups=mesh['blk'=64,'body'=8] {'blk'}, dimensions={0} | all-to-all | bytes 786432 | tf_op jit(solution)/shard_map/all_to_all | solution.py:368
  60.1 0.9 %finish.1 = (f32[3,2048]{1,0:T(4,128)}, f32[3,2048]{1,0:T(4,128)}) custom-call(s32[133]{0:T(256)S(4)} %get-tuple-element.13.plan_ref, f32[768,128]{1,0:T(8,128)S(1)} %bitcast.5, f32[16,8,128]{2,1,0:T(8,128)S(1)} %get-tuple-element.23.terms_ref), custom_call_target="tpu_custom_call" | custom-call | tf_op jit(solution)/shard_map/finish/pallas_call | solution.py:427
Async XLA Ops:
  3.3 17.2 %copy-start = (f32[3,2048]{1,0:T(4,128)S(1)}, f32[3,2048]{1,0:T(4,128)}, u32[]{:S(2)}) copy-start(f32[3,2048]{1,0:T(4,128)} %pos_ref.3) | copy-start | bytes 73732
  3.3 17.2 %copy-start.1 = (f32[3,2048]{1,0:T(4,128)S(1)}, f32[3,2048]{1,0:T(4,128)}, u32[]{:S(2)}) copy-start(f32[3,2048]{1,0:T(4,128)} %dir_ref.3) | copy-start | bytes 73732
  3.3 26.2 %all-to-all-start = ((f32[64,13,1,128]{3,2,1,0:T(1,128)}), f32[64,13,1,128]{3,2,1,0:T(1,128)S(1)}, u32[]{:S(2)}, u32[]{:S(2)}) async-start(f32[64,13,1,128]{3,2,1,0:T(1,128)} %bitcast), calls=%async_computation | async-start | bytes 851968 | tf_op jit(solution)/shard_map/all_to_all | solution.py:368
  14.5 6.1 %copy-start.2 = (s32[8]{0:T(128)S(1)}, s32[8]{0:T(128)}, u32[]{:S(2)}) copy-start(s32[8]{0:T(128)} %local_ref.3) | copy-start | bytes 100
  14.5 6.1 %copy-start.3 = (s32[8]{0:T(128)S(1)}, s32[8]{0:T(128)}, u32[]{:S(2)}) copy-start(s32[8]{0:T(128)} %face_ref.3) | copy-start | bytes 100
  14.5 6.0 %collective-permute-start = (f32[24,128]{1,0:T(8,128)S(1)}, f32[24,128]{1,0:T(8,128)S(1)}, u32[]{:S(2)}, u32[]{:S(2)}) collective-permute-start(f32[24,128]{1,0:T(8,128)S(1)} %get-tuple-element.15), channel_id=1, source_target_pairs={{0,1},{1,2},{2,3},{3,4},{4,5},{5,6},{6,7},{8,9},{9,10},{10,11},{11... | collective-permute-start | bytes 36872 | tf_op jit(solution)/shard_map/ppermute | solution.py:29
  22.6 6.5 %collective-permute-start.1 = (f32[24,128]{1,0:T(8,128)S(1)}, f32[24,128]{1,0:T(8,128)S(1)}, u32[]{:S(2)}, u32[]{:S(2)}) collective-permute-start(f32[24,128]{1,0:T(8,128)S(1)} %get-tuple-element.16), channel_id=1, source_target_pairs={{1,0},{2,1},{3,2},{4,3},{5,4},{6,5},{7,6},{9,8},{10,9},{11,10},{12... | collective-permute-start | bytes 36872 | tf_op jit(solution)/shard_map/ppermute | solution.py:29

commit v3 on v2

--- a/solution.py
+++ b/solution.py
@@ -1,5 +1,3 @@
-import functools
-
 import jax
 import jax.numpy as jnp
 from jax import lax
@@ -220,7 +218,7 @@
 
 
 def main_kernel(
-    plan_ref, arrived_ref, back_ref, sums_in_ref, rows_ref, feature_ref, left_ref, center_ref,
+    arrived_ref, sums_in_ref, rows_ref, feature_ref, left_ref, center_ref,
     return_ref, terms_ref,
     sums_ref, list_ref, table_ref, sem,
     *buffers,
@@ -313,20 +311,20 @@
 
     for block in range(num_blocks):
         terms_ref[block] = own_terms(rows_ref[block], sums_ref[block])
-    faces = back_ref.shape[0] // SIX
-    for face in range(faces):
-        block = plan_ref[plan_ref.shape[0] - faces + face]
-        terms_ref[block, 0:SIX, :] += back_ref[face * SIX : face * SIX + SIX, :]
 
 
 def finish_kernel(
-    num_pairs, plan_ref, returned_ref, terms_ref,
+    plan_ref, returned_ref, terms_ref, back_ref,
     grad_ref, hess_ref,
     total_ref,
 ):
     num_blocks = terms_ref.shape[0]
-    pairs = num_pairs
+    faces = back_ref.shape[0] // SIX
+    pairs = (plan_ref.shape[0] - 1 - faces) // 2
     total_ref[0:num_blocks] = terms_ref[...]
+    for face in range(faces):
+        block = plan_ref[2 * pairs + 1 + face]
+        total_ref[block, 0:SIX, :] += back_ref[face * SIX : face * SIX + SIX, :]
     count = plan_ref[2 * pairs]
 
     def some(step, carry):
@@ -411,7 +409,7 @@
         name="pairs",
         compiler_params=limit(8),
         out_shape=(on_chip(peers * RET, LANES), on_chip(num_blocks, 8, LANES)),
-        in_specs=[smem()] + [vmem()] * 7,
+        in_specs=[vmem()] * 6,
         out_specs=(vmem(), vmem()),
         scratch_shapes=[
             pltpu.VMEM((num_blocks + 1, 8, 2 * LANES), F32),
@@ -422,16 +420,16 @@
         + [pltpu.VMEM((GROUP, 2 * LANES, LANES), F32)] * IN_TURN
         + [pltpu.VMEM((GROUP, 32, LANES), BF16)] * IN_TURN
         + [pltpu.VMEM((GROUP, 8, LANES), F32)] * IN_TURN,
-    )(plan, *held(arrived, face_back, sums, *local))
+    )(*held(arrived, sums, *local))
     returned = exchange(outgoing, peers)
     return pl.pallas_call(
-        functools.partial(finish_kernel, pair_local.shape[0]),
+        finish_kernel,
         name="finish",
         out_shape=[jax.ShapeDtypeStruct((3, num_blocks * LANES), F32)] * 2,
-        in_specs=[smem()] + [vmem()] * 2,
+        in_specs=[smem()] + [vmem()] * 3,
         out_specs=(vmem(), vmem()),
         scratch_shapes=[pltpu.VMEM((num_blocks + 1, 8, LANES), F32)],
-    )(plan, *held(returned, terms))
+    )(plan, *held(returned, terms, face_back))
 
 
 def solution(mesh):

time: 61.1 us -> 58 us (0.949)
  the two profiles are of different devices: /device:TPU:199 before, /device:TPU:1 now
where the time goes in v3:
time: 58 us; the launch traced here: 57.3 us
  waiting for transfers between devices  23.5 us (41%)
  starting transfers between devices  23.3 us (40%)
  Pallas kernels  9.08 us (16%)
  between operations  1.34 us (2%)
    all_to_all x2, waiting for transfers between devices, exchange(): lax.all_to_all(rows.reshape(peers, count, 1, LANES), 'blk', split_axis=0,...  18.7 us
    all_to_all x2, starting transfers between devices, exchange(): lax.all_to_all(rows.reshape(peers, count, 1, LANES), 'blk', split_axis=0,...  18.1 us
    pallas_call x1, Pallas kernels, per_device(): pl.pallas_call(main_kernel, name='pairs', compiler_params=limit(8), out_s...  5.36 us
    ppermute x2, starting transfers between devices, from_behind(): lax.ppermute(value, axis, [(source, source + steps) for source in range(f...  5.25 us
    ppermute x2, waiting for transfers between devices, from_behind(): lax.ppermute(value, axis, [(source, source + steps) for source in range(f...  4.84 us
    pallas_call x1, Pallas kernels, per_device(): pl.pallas_call(pack_kernel, name='pack', out_shape=(on_chip(peers * MSG,...  1.92 us
  transfers between devices with their start and end apart: 4, of which 4 were waited for; matrix products, arithmetic and copies ran while one was open for 0% of the time, Pallas kernels for 2%

profile of v3, /device:TPU:1, one launch (start us, length us, event | category | flops | bytes accessed | tf_op | source)
XLA Modules:
  0.0 57.3 jit_solution(14524977367141415070)
XLA Ops:
  1.3 1.9 %pack.1 = (f32[832,128]{1,0:T(8,128)}, f32[24,128]{1,0:T(8,128)S(1)}, s32[133]{0:T(256)S(4)}) custom-call(s32[64]{0:T(128)} %local_ref.2, s32[64]{0:T(128)} %peer_ref.1, s32[64]{0:T(128)} %shift_ref.1, s32[1]{0:T(128)S(6)} %copy.13.count_ref, s32[4]{0:T(128)} %face_ref.2, f32[3,2048]{1,0:T(4,128)} %pos_ref.3, f32[3,2048]{1,0:T(4,128)} %dir_ref.3), custom_call_target="tpu_custom_call" | custom-call | tf_op jit(solution)/shard_map/pack/pallas_call | solution.py:384
  3.2 0.0 copy-start
  3.2 0.0 copy-start.1
  3.2 11.8 %all-to-all-start = ((f32[64,13,1,128]{3,2,1,0:T(1,128)}), f32[64,13,1,128]{3,2,1,0:T(1,128)S(1)}, u32[]{:S(2)}, u32[]{:S(2)}) async-start(f32[64,13,1,128]{3,2,1,0:T(1,128)} %bitcast), calls=%async_computation | async-start | bytes 851968 | tf_op jit(solution)/shard_map/all_to_all | solution.py:366
  15.0 0.0 copy-start.2
  15.0 0.0 copy-start.3
  15.0 4.0 %collective-permute-start = (f32[24,128]{1,0:T(8,128)S(1)}, f32[24,128]{1,0:T(8,128)S(1)}, u32[]{:S(2)}, u32[]{:S(2)}) collective-permute-start(f32[24,128]{1,0:T(8,128)S(1)} %get-tuple-element.15), channel_id=1, source_target_pairs={{0,1},{1,2},{2,3},{3,4},{4,5},{5,6},{6,7},{8,9},{9,10},{10,11},{11... | collective-permute-start | bytes 36872 | tf_op jit(solution)/shard_map/ppermute | solution.py:27
  19.0 0.8 %collective-permute-done.incoming_ref = f32[24,128]{1,0:T(8,128)S(1)} collective-permute-done((f32[24,128]{1,0:T(8,128)S(1)}, f32[24,128]{1,0:T(8,128)S(1)}, u32[]{:S(2)}, u32[]{:S(2)}) %collective-permute-start) | collective-permute-done | bytes 12320 | tf_op jit(solution)/shard_map/ppermute | solution.py:27
  19.8 0.0 copy-done
  19.8 0.0 copy-done.1
  19.8 0.0 copy-done.2
  19.8 0.0 copy-done.3
  19.8 1.0 %cross.1 = (f32[16,8,256]{2,1,0:T(8,128)S(1)}, f32[24,128]{1,0:T(8,128)S(1)}, f32[16,8,128]{2,1,0:T(8,128)S(1)}, bf16[16,256,128]{2,1,0:T(8,128)(2,1)S(1)}, bf16...) custom-call(s32[8]{0:T(128)S(1)} %copy-done.2, s32[8]{0:T(128)S(1)} %copy-done.3, f32[3,2048]{1,0:T(4,128)S(1)} %copy-done, ...), custom_call_target="tpu_custom_call" | custom-call | tf_op jit(solution)/shard_map/cross/pallas_call | solution.py:398
  20.9 9.4 %all-to-all-done = f32[64,13,1,128]{3,2,1,0:T(1,128)S(1)} async-done(((f32[64,13,1,128]{3,2,1,0:T(1,128)}), f32[64,13,1,128]{3,2,1,0:T(1,128)S(1)}, u32[]{:S(2)}, u32[]{:S(2)}) %all-to-all-start) | async-done | bytes 426016 | tf_op jit(solution)/shard_map/all_to_all | solution.py:366
  30.3 5.4 %pairs.1 = (f32[768,128]{1,0:T(8,128)}, f32[16,8,128]{2,1,0:T(8,128)S(1)}) custom-call(f32[832,128]{1,0:T(8,128)S(1)} %bitcast.4, f32[16,8,256]{2,1,0:T(8,128)S(1)} %get-tuple-element.16.sums_in_ref, f32[16,8,128]{2,1,0:T(8,128)S(1)} %get-tuple-element.17.rows_ref, bf16[16,256,128]{2,1,0:T(8,128)(2,1)S(1)} %get-tuple-element.18.feature_ref, ...), custom_call_target="tpu_custom_call" | custom-call | tf_op jit(solution)/shard_map/pairs/pallas_call | solution.py:407
  35.7 6.2 %all-to-all-start.1 = ((f32[64,12,1,128]{3,2,1,0:T(1,128)}), f32[64,12,1,128]{3,2,1,0:T(1,128)S(1)}, u32[]{:S(2)}, u32[]{:S(2)}) async-start(f32[64,12,1,128]{3,2,1,0:T(1,128)} %bitcast.2), calls=%async_computation.1 | async-start | bytes 786432 | tf_op jit(solution)/shard_map/all_to_all | solution.py:366
  41.9 1.3 %collective-permute-start.1 = (f32[24,128]{1,0:T(8,128)S(1)}, f32[24,128]{1,0:T(8,128)S(1)}, u32[]{:S(2)}, u32[]{:S(2)}) collective-permute-start(f32[24,128]{1,0:T(8,128)S(1)} %get-tuple-element.23), channel_id=1, source_target_pairs={{1,0},{2,1},{3,2},{4,3},{5,4},{6,5},{7,6},{9,8},{10,9},{11,10},{12... | collective-permute-start | bytes 36872 | tf_op jit(solution)/shard_map/ppermute | solution.py:27
  43.2 4.0 %collective-permute-done.1.back_ref = f32[24,128]{1,0:T(8,128)S(1)} collective-permute-done((f32[24,128]{1,0:T(8,128)S(1)}, f32[24,128]{1,0:T(8,128)S(1)}, u32[]{:S(2)}, u32[]{:S(2)}) %collective-permute-start.1) | collective-permute-done | bytes 12320 | tf_op jit(solution)/shard_map/ppermute | solution.py:27
  47.2 9.2 %all-to-all-done.1 = f32[64,12,1,128]{3,2,1,0:T(1,128)S(1)} async-done(((f32[64,12,1,128]{3,2,1,0:T(1,128)}), f32[64,12,1,128]{3,2,1,0:T(1,128)S(1)}, u32[]{:S(2)}, u32[]{:S(2)}) %all-to-all-start.1) | async-done | bytes 393248 | tf_op jit(solution)/shard_map/all_to_all | solution.py:366
  56.4 0.8 %finish.1 = (f32[3,2048]{1,0:T(4,128)}, f32[3,2048]{1,0:T(4,128)}) custom-call(s32[133]{0:T(256)S(4)} %get-tuple-element.13.plan_ref, f32[768,128]{1,0:T(8,128)S(1)} %bitcast.5, f32[16,8,128]{2,1,0:T(8,128)S(1)} %get-tuple-element.22.terms_ref, f32[24,128]{1,0:T(8,128)S(1)} %collective-permute-done.1.back_ref), custom_call_target="tpu_custom_call" | custom-call | tf_op jit(solution)/shard_map/finish/pallas_call | solution.py:425
Async XLA Ops:
  3.2 16.6 %copy-start = (f32[3,2048]{1,0:T(4,128)S(1)}, f32[3,2048]{1,0:T(4,128)}, u32[]{:S(2)}) copy-start(f32[3,2048]{1,0:T(4,128)} %pos_ref.3) | copy-start | bytes 73732
  3.2 16.6 %copy-start.1 = (f32[3,2048]{1,0:T(4,128)S(1)}, f32[3,2048]{1,0:T(4,128)}, u32[]{:S(2)}) copy-start(f32[3,2048]{1,0:T(4,128)} %dir_ref.3) | copy-start | bytes 73732
  3.2 27.1 %all-to-all-start = ((f32[64,13,1,128]{3,2,1,0:T(1,128)}), f32[64,13,1,128]{3,2,1,0:T(1,128)S(1)}, u32[]{:S(2)}, u32[]{:S(2)}) async-start(f32[64,13,1,128]{3,2,1,0:T(1,128)} %bitcast), calls=%async_computation | async-start | bytes 851968 | tf_op jit(solution)/shard_map/all_to_all | solution.py:366
  15.0 4.8 %copy-start.2 = (s32[8]{0:T(128)S(1)}, s32[8]{0:T(128)}, u32[]{:S(2)}) copy-start(s32[8]{0:T(128)} %local_ref.3) | copy-start | bytes 100
  15.0 4.8 %copy-start.3 = (s32[8]{0:T(128)S(1)}, s32[8]{0:T(128)}, u32[]{:S(2)}) copy-start(s32[8]{0:T(128)} %face_ref.3) | copy-start | bytes 100
  15.0 4.8 %collective-permute-start = (f32[24,128]{1,0:T(8,128)S(1)}, f32[24,128]{1,0:T(8,128)S(1)}, u32[]{:S(2)}, u32[]{:S(2)}) collective-permute-start(f32[24,128]{1,0:T(8,128)S(1)} %get-tuple-element.15), channel_id=1, source_target_pairs={{0,1},{1,2},{2,3},{3,4},{4,5},{5,6},{6,7},{8,9},{9,10},{10,11},{11... | collective-permute-start | bytes 36872 | tf_op jit(solution)/shard_map/ppermute | solution.py:27
  35.7 20.8 %all-to-all-start.1 = ((f32[64,12,1,128]{3,2,1,0:T(1,128)}), f32[64,12,1,128]{3,2,1,0:T(1,128)S(1)}, u32[]{:S(2)}, u32[]{:S(2)}) async-start(f32[64,12,1,128]{3,2,1,0:T(1,128)} %bitcast.2), calls=%async_computation.1 | async-start | bytes 786432 | tf_op jit(solution)/shard_map/all_to_all | solution.py:366
  41.9 5.3 %collective-permute-start.1 = (f32[24,128]{1,0:T(8,128)S(1)}, f32[24,128]{1,0:T(8,128)S(1)}, u32[]{:S(2)}, u32[]{:S(2)}) collective-permute-start(f32[24,128]{1,0:T(8,128)S(1)} %get-tuple-element.23), channel_id=1, source_target_pairs={{1,0},{2,1},{3,2},{4,3},{5,4},{6,5},{7,6},{9,8},{10,9},{11,10},{12... | collective-permute-start | bytes 36872 | tf_op jit(solution)/shard_map/ppermute | solution.py:27

commit v4 on v3

--- a/solution.py
+++ b/solution.py
@@ -5,10 +5,12 @@
 from jax.experimental.pallas import tpu as pltpu
 from jax.sharding import PartitionSpec as P
 
+
 XI = 0.1
 TWICE_LN2 = 1.3862943611198906
 SCALE = 0.02
 LANES = 128
+FACES = 4
 SIX = 6
 MSG = 13
 RET = 12
@@ -27,15 +29,9 @@
     return lax.ppermute(value, axis, [(source, source + steps) for source in range(first, last)])
 
 
-def put_block(target_ref, start, pos_ref, dir_ref, block):
-    cols = pl.ds(pl.multiple_of(block * LANES, LANES), LANES)
-    target_ref[pl.ds(start, 3), :] = pos_ref[:, cols]
-    target_ref[pl.ds(start + 3, 3), :] = dir_ref[:, cols]
-
-
 def pack_kernel(
     local_ref, peer_ref, shift_ref, count_ref, face_ref, pos_ref, dir_ref,
-    send_ref, faces_ref, plan_ref, used_ref,
+    send_ref, faces_ref, plan_ref, used_ref, block_ref,
 ):
     peers = used_ref.shape[0]
     pairs = local_ref.shape[0]
@@ -43,6 +39,10 @@
     count = count_ref[0]
     lane = lax.broadcasted_iota(jnp.int32, (1, LANES), 1)
     unused = jnp.full((1, LANES), -1.0, F32)
+    for block in range(num_blocks):
+        span = slice(block * LANES, (block + 1) * LANES)
+        block_ref[block, 0:3, :] = pos_ref[:, span]
+        block_ref[block, 3:6, :] = dir_ref[:, span]
     for peer in range(peers):
         used_ref[peer] = 0
         row = peer * MSG + RET
@@ -53,13 +53,14 @@
             pair = step * UNROLL + k
             near = local_ref[pair]
             peer = peer_ref[pair]
-            far = lax.rem(near + shift_ref[pair], num_blocks)
+            far = jnp.bitwise_and(near + shift_ref[pair], num_blocks - 1)
             mark = jnp.where(pair < count, far, -1).astype(F32)
             rank = used_ref[peer]
             used_ref[peer] = rank + 1
-            plan_ref[pair] = peer * RET + rank * SIX
+            row = peer * RET + rank * SIX
+            plan_ref[pair] = row
             plan_ref[pairs + pair] = near
-            put_block(send_ref, peer * MSG + rank * SIX, pos_ref, dir_ref, near)
+            send_ref[pl.ds(row + peer, SIX), :] = block_ref[near, 0:SIX, :]
             pltpu.store(
                 send_ref.at[pl.ds(peer * MSG + RET, 1), :],
                 jnp.broadcast_to(mark, (1, LANES)),
@@ -72,7 +73,7 @@
     for face in range(face_ref.shape[0]):
         block = face_ref[face]
         plan_ref[2 * pairs + 1 + face] = block
-        put_block(faces_ref, face * SIX, pos_ref, dir_ref, block)
+        faces_ref[face * SIX : face * SIX + SIX, :] = block_ref[block, 0:SIX, :]
 
 
 def pieces(value):
@@ -313,18 +314,10 @@
         terms_ref[block] = own_terms(rows_ref[block], sums_ref[block])
 
 
-def finish_kernel(
-    plan_ref, returned_ref, terms_ref, back_ref,
-    grad_ref, hess_ref,
-    total_ref,
-):
+def gather_kernel(plan_ref, returned_ref, terms_ref, total_ref):
     num_blocks = terms_ref.shape[0]
-    faces = back_ref.shape[0] // SIX
-    pairs = (plan_ref.shape[0] - 1 - faces) // 2
+    pairs = (plan_ref.shape[0] - 1 - FACES) // 2
     total_ref[0:num_blocks] = terms_ref[...]
-    for face in range(faces):
-        block = plan_ref[2 * pairs + 1 + face]
-        total_ref[block, 0:SIX, :] += back_ref[face * SIX : face * SIX + SIX, :]
     count = plan_ref[2 * pairs]
 
     def some(step, carry):
@@ -335,10 +328,17 @@
         return carry
 
     lax.fori_loop(0, (count + UNROLL - 1) // UNROLL, some, 0)
-    for block in range(num_blocks):
+
+
+def finish_kernel(plan_ref, total_ref, back_ref, grad_ref, hess_ref, sum_ref):
+    sum_ref[...] = total_ref[...]
+    for face in range(FACES):
+        block = plan_ref[plan_ref.shape[0] - FACES + face]
+        sum_ref[block, 0:SIX, :] += back_ref[face * SIX : face * SIX + SIX, :]
+    for block in range(sum_ref.shape[0] - 1):
         span = slice(block * LANES, (block + 1) * LANES)
-        grad_ref[:, span] = SCALE * total_ref[block, 0:3, :]
-        hess_ref[:, span] = SCALE * total_ref[block, 3:6, :]
+        grad_ref[:, span] = SCALE * sum_ref[block, 0:3, :]
+        hess_ref[:, span] = SCALE * sum_ref[block, 3:6, :]
 
 
 def smem():
@@ -391,7 +391,10 @@
         ),
         in_specs=[smem()] * 5 + [vmem()] * 2,
         out_specs=(vmem(), vmem(), smem()),
-        scratch_shapes=[pltpu.SMEM((peers,), jnp.int32)],
+        scratch_shapes=[
+            pltpu.SMEM((peers,), jnp.int32),
+            pltpu.VMEM((num_blocks, 8, LANES), F32),
+        ],
     )(pair_local, pair_peer, pair_shift, pair_count, face_index, positions, direction)
     arrived = exchange(send, peers)
     incoming = from_behind(face_rows, "body", 1)
@@ -422,19 +425,28 @@
         + [pltpu.VMEM((GROUP, 8, LANES), F32)] * IN_TURN,
     )(*held(arrived, sums, *local))
     returned = exchange(outgoing, peers)
+    total = pl.pallas_call(
+        gather_kernel,
+        name="gather",
+        compiler_params=limit(8),
+        out_shape=on_chip(num_blocks + 1, 8, LANES),
+        in_specs=[smem()] + [vmem()] * 2,
+        out_specs=vmem(),
+    )(plan, *held(returned, terms))
     return pl.pallas_call(
         finish_kernel,
         name="finish",
         out_shape=[jax.ShapeDtypeStruct((3, num_blocks * LANES), F32)] * 2,
-        in_specs=[smem()] + [vmem()] * 3,
+        in_specs=[smem()] + [vmem()] * 2,
         out_specs=(vmem(), vmem()),
         scratch_shapes=[pltpu.VMEM((num_blocks + 1, 8, LANES), F32)],
-    )(plan, *held(returned, terms, face_back))
+    )(plan, *held(total, face_back))
 
 
 def solution(mesh):
     split_all = P(("blk", "body"))
     wide = P(None, ("blk", "body"))
+
     return jax.shard_map(
         per_device,
         mesh=mesh,

time: 58 us -> 57.6 us (level)
    ppermute x2, waiting for transfers between devices: 4.84 us -> 0.82 us  [from_behind(): lax.ppermute(value, axis, [(source, source + steps) for source in range(f...]
    all_to_all x2, waiting for transfers between devices: 18.7 us -> 22.6 us  [exchange(): lax.all_to_all(rows.reshape(peers, count, 1, LANES), 'blk', split_axis=0,...]
  transfers between devices with their start and end apart: 4 -> 4, of which waited for: 4 -> 3; matrix products, arithmetic and copies ran while one was open for 0% -> 0% of each run, Pallas kernels for 2% -> 2%
where the time goes in v4:
time: 57.6 us; the launch traced here: 57.2 us
  waiting for transfers between devices  23.4 us (41%)
  starting transfers between devices  23.3 us (40%)
  Pallas kernels  9.13 us (16%)
  between operations  1.36 us (2%)
    all_to_all x2, waiting for transfers between devices, exchange(): lax.all_to_all(rows.reshape(peers, count, 1, LANES), 'blk', split_axis=0,...  22.6 us
    all_to_all x2, starting transfers between devices, exchange(): lax.all_to_all(rows.reshape(peers, count, 1, LANES), 'blk', split_axis=0,...  18 us
    pallas_call x1, Pallas kernels, per_device(): pl.pallas_call(main_kernel, name='pairs', compiler_params=limit(8), out_s...  5.36 us
    ppermute x2, starting transfers between devices, from_behind(): lax.ppermute(value, axis, [(source, source + steps) for source in range(f...  5.32 us
    pallas_call x1, Pallas kernels, per_device(): pl.pallas_call(pack_kernel, name='pack', out_shape=(on_chip(peers * MSG,...  1.92 us
  transfers between devices with their start and end apart: 4, of which 3 were waited for; matrix products, arithmetic and copies ran while one was open for 0% of the time, Pallas kernels for 2%

profile of v4, /device:TPU:1, one launch (start us, length us, event | category | flops | bytes accessed | tf_op | source)
XLA Modules:
  0.0 57.2 jit_solution(15919061933251830530)
XLA Ops:
  1.3 1.9 %pack.1 = (f32[832,128]{1,0:T(8,128)}, f32[24,128]{1,0:T(8,128)S(1)}, s32[133]{0:T(256)S(4)}) custom-call(s32[64]{0:T(128)} %local_ref.2, s32[64]{0:T(128)} %peer_ref.1, s32[64]{0:T(128)} %shift_ref.1, s32[1]{0:T(128)S(6)} %copy.13.count_ref, s32[4]{0:T(128)} %face_ref.2, f32[3,2048]{1,0:T(4,128)} %pos_ref.3, f32[3,2048]{1,0:T(4,128)} %dir_ref.3), custom_call_target="tpu_custom_call" | custom-call | tf_op jit(solution)/shard_map/pack/pallas_call | solution.py:384
  3.2 0.0 copy-start
  3.2 0.0 copy-start.1
  3.2 11.7 %all-to-all-start = ((f32[64,13,1,128]{3,2,1,0:T(1,128)}), f32[64,13,1,128]{3,2,1,0:T(1,128)S(1)}, u32[]{:S(2)}, u32[]{:S(2)}) async-start(f32[64,13,1,128]{3,2,1,0:T(1,128)} %bitcast), calls=%async_computation | async-start | bytes 851968 | tf_op jit(solution)/shard_map/all_to_all | solution.py:366
  14.9 0.0 copy-start.2
  15.0 0.0 copy-start.3
  15.0 4.0 %collective-permute-start = (f32[24,128]{1,0:T(8,128)S(1)}, f32[24,128]{1,0:T(8,128)S(1)}, u32[]{:S(2)}, u32[]{:S(2)}) collective-permute-start(f32[24,128]{1,0:T(8,128)S(1)} %get-tuple-element.15), channel_id=1, source_target_pairs={{0,1},{1,2},{2,3},{3,4},{4,5},{5,6},{6,7},{8,9},{9,10},{10,11},{11... | collective-permute-start | bytes 36872 | tf_op jit(solution)/shard_map/ppermute | solution.py:29
  19.0 0.8 %collective-permute-done.incoming_ref = f32[24,128]{1,0:T(8,128)S(1)} collective-permute-done((f32[24,128]{1,0:T(8,128)S(1)}, f32[24,128]{1,0:T(8,128)S(1)}, u32[]{:S(2)}, u32[]{:S(2)}) %collective-permute-start) | collective-permute-done | bytes 12320 | tf_op jit(solution)/shard_map/ppermute | solution.py:29
  19.8 0.0 copy-done
  19.8 0.0 copy-done.1
  19.8 0.0 copy-done.2
  19.8 0.0 copy-done.3
  19.8 1.0 %cross.1 = (f32[16,8,256]{2,1,0:T(8,128)S(1)}, f32[24,128]{1,0:T(8,128)S(1)}, f32[16,8,128]{2,1,0:T(8,128)S(1)}, bf16[16,256,128]{2,1,0:T(8,128)(2,1)S(1)}, bf16...) custom-call(s32[8]{0:T(128)S(1)} %copy-done.2, s32[8]{0:T(128)S(1)} %copy-done.3, f32[3,2048]{1,0:T(4,128)S(1)} %copy-done, ...), custom_call_target="tpu_custom_call" | custom-call | tf_op jit(solution)/shard_map/cross/pallas_call | solution.py:401
  20.8 9.4 %all-to-all-done = f32[64,13,1,128]{3,2,1,0:T(1,128)S(1)} async-done(((f32[64,13,1,128]{3,2,1,0:T(1,128)}), f32[64,13,1,128]{3,2,1,0:T(1,128)S(1)}, u32[]{:S(2)}, u32[]{:S(2)}) %all-to-all-start) | async-done | bytes 426016 | tf_op jit(solution)/shard_map/all_to_all | solution.py:366
  30.2 5.4 %pairs.1 = (f32[768,128]{1,0:T(8,128)}, f32[16,8,128]{2,1,0:T(8,128)S(1)}) custom-call(f32[832,128]{1,0:T(8,128)S(1)} %bitcast.4, f32[16,8,256]{2,1,0:T(8,128)S(1)} %get-tuple-element.16.sums_in_ref, f32[16,8,128]{2,1,0:T(8,128)S(1)} %get-tuple-element.17.rows_ref, bf16[16,256,128]{2,1,0:T(8,128)(2,1)S(1)} %get-tuple-element.18.feature_ref, ...), custom_call_target="tpu_custom_call" | custom-call | tf_op jit(solution)/shard_map/pairs/pallas_call | solution.py:410
  35.6 6.2 %all-to-all-start.1 = ((f32[64,12,1,128]{3,2,1,0:T(1,128)}), f32[64,12,1,128]{3,2,1,0:T(1,128)S(1)}, u32[]{:S(2)}, u32[]{:S(2)}) async-start(f32[64,12,1,128]{3,2,1,0:T(1,128)} %bitcast.2), calls=%async_computation.1 | async-start | bytes 786432 | tf_op jit(solution)/shard_map/all_to_all | solution.py:366
  41.8 1.3 %collective-permute-start.1 = (f32[24,128]{1,0:T(8,128)S(1)}, f32[24,128]{1,0:T(8,128)S(1)}, u32[]{:S(2)}, u32[]{:S(2)}) collective-permute-start(f32[24,128]{1,0:T(8,128)S(1)} %get-tuple-element.23), channel_id=1, source_target_pairs={{1,0},{2,1},{3,2},{4,3},{5,4},{6,5},{7,6},{9,8},{10,9},{11,10},{12... | collective-permute-start | bytes 36872 | tf_op jit(solution)/shard_map/ppermute | solution.py:29
  43.1 13.2 %all-to-all-done.1 = f32[64,12,1,128]{3,2,1,0:T(1,128)S(1)} async-done(((f32[64,12,1,128]{3,2,1,0:T(1,128)}), f32[64,12,1,128]{3,2,1,0:T(1,128)S(1)}, u32[]{:S(2)}, u32[]{:S(2)}) %all-to-all-start.1) | async-done | bytes 393248 | tf_op jit(solution)/shard_map/all_to_all | solution.py:366
  56.4 0.2 gather.1.total_ref
  56.6 0.0 collective-permute-done.1.back_ref
  56.6 0.7 %finish.1 = (f32[3,2048]{1,0:T(4,128)}, f32[3,2048]{1,0:T(4,128)}) custom-call(s32[133]{0:T(256)S(4)} %get-tuple-element.13.plan_ref, f32[17,8,128]{2,1,0:T(8,128)S(1)} %gather.1.total_ref, f32[24,128]{1,0:T(8,128)S(1)} %collective-permute-done.1.back_ref), custom_call_target="tpu_custom_call" | custom-call | tf_op jit(solution)/shard_map/finish/pallas_call | solution.py:436
Async XLA Ops:
  3.2 16.6 %copy-start = (f32[3,2048]{1,0:T(4,128)S(1)}, f32[3,2048]{1,0:T(4,128)}, u32[]{:S(2)}) copy-start(f32[3,2048]{1,0:T(4,128)} %pos_ref.3) | copy-start | bytes 73732
  3.2 16.6 %copy-start.1 = (f32[3,2048]{1,0:T(4,128)S(1)}, f32[3,2048]{1,0:T(4,128)}, u32[]{:S(2)}) copy-start(f32[3,2048]{1,0:T(4,128)} %dir_ref.3) | copy-start | bytes 73732
  3.2 27.0 %all-to-all-start = ((f32[64,13,1,128]{3,2,1,0:T(1,128)}), f32[64,13,1,128]{3,2,1,0:T(1,128)S(1)}, u32[]{:S(2)}, u32[]{:S(2)}) async-start(f32[64,13,1,128]{3,2,1,0:T(1,128)} %bitcast), calls=%async_computation | async-start | bytes 851968 | tf_op jit(solution)/shard_map/all_to_all | solution.py:366
  14.9 4.9 %copy-start.2 = (s32[8]{0:T(128)S(1)}, s32[8]{0:T(128)}, u32[]{:S(2)}) copy-start(s32[8]{0:T(128)} %local_ref.3) | copy-start | bytes 100
  15.0 4.9 %copy-start.3 = (s32[8]{0:T(128)S(1)}, s32[8]{0:T(128)}, u32[]{:S(2)}) copy-start(s32[8]{0:T(128)} %face_ref.3) | copy-start | bytes 100
  15.0 4.8 %collective-permute-start = (f32[24,128]{1,0:T(8,128)S(1)}, f32[24,128]{1,0:T(8,128)S(1)}, u32[]{:S(2)}, u32[]{:S(2)}) collective-permute-start(f32[24,128]{1,0:T(8,128)S(1)} %get-tuple-element.15), channel_id=1, source_target_pairs={{0,1},{1,2},{2,3},{3,4},{4,5},{5,6},{6,7},{8,9},{9,10},{10,11},{11... | collective-permute-start | bytes 36872 | tf_op jit(solution)/shard_map/ppermute | solution.py:29
  35.6 20.8 %all-to-all-start.1 = ((f32[64,12,1,128]{3,2,1,0:T(1,128)}), f32[64,12,1,128]{3,2,1,0:T(1,128)S(1)}, u32[]{:S(2)}, u32[]{:S(2)}) async-start(f32[64,12,1,128]{3,2,1,0:T(1,128)} %bitcast.2), calls=%async_computation.1 | async-start | bytes 786432 | tf_op jit(solution)/shard_map/all_to_all | solution.py:366
  41.8 14.7 %collective-permute-start.1 = (f32[24,128]{1,0:T(8,128)S(1)}, f32[24,128]{1,0:T(8,128)S(1)}, u32[]{:S(2)}, u32[]{:S(2)}) collective-permute-start(f32[24,128]{1,0:T(8,128)S(1)} %get-tuple-element.23), channel_id=1, source_target_pairs={{1,0},{2,1},{3,2},{4,3},{5,4},{6,5},{7,6},{9,8},{10,9},{11,10},{12... | collective-permute-start | bytes 36872 | tf_op jit(solution)/shard_map/ppermute | solution.py:29

commit v5 on v4

--- a/solution.py
+++ b/solution.py
@@ -38,7 +38,8 @@
     num_blocks = pos_ref.shape[1] // LANES
     count = count_ref[0]
     lane = lax.broadcasted_iota(jnp.int32, (1, LANES), 1)
-    unused = jnp.full((1, LANES), -1.0, F32)
+    mine = lax.axis_index("blk")
+    unused = jnp.zeros((1, LANES), F32)
     for block in range(num_blocks):
         span = slice(block * LANES, (block + 1) * LANES)
         block_ref[block, 0:3, :] = pos_ref[:, span]
@@ -54,7 +55,7 @@
             near = local_ref[pair]
             peer = peer_ref[pair]
             far = jnp.bitwise_and(near + shift_ref[pair], num_blocks - 1)
-            mark = jnp.where(pair < count, far, -1).astype(F32)
+            mark = jnp.where(pair < count, far + 1, 0).astype(F32)
             rank = used_ref[peer]
             used_ref[peer] = rank + 1
             row = peer * RET + rank * SIX
@@ -64,7 +65,7 @@
             pltpu.store(
                 send_ref.at[pl.ds(peer * MSG + RET, 1), :],
                 jnp.broadcast_to(mark, (1, LANES)),
-                mask=lane == rank,
+                mask=lane == rank * peers + mine,
             )
         return carry
 
@@ -227,13 +228,8 @@
     peers = arrived_ref.shape[0] // MSG
     slots = 2 * peers
     num_blocks = terms_ref.shape[0]
-    marks = arrived_ref[pl.ds(RET, peers, stride=MSG), :].astype(BF16)
-    pick = (
-        lax.broadcasted_iota(jnp.int32, (16, LANES), 0)
-        == lax.broadcasted_iota(jnp.int32, (16, LANES), 1)
-    ).astype(BF16)
-    found = lax.dot_general(pick, marks, NT, preferred_element_type=F32)
-    wide = jnp.concatenate([found[0:1], found[1:2]], axis=1)
+    marks = arrived_ref[pl.ds(RET, peers, stride=MSG), :]
+    wide = jnp.sum(marks, axis=0, keepdims=True)[:, :slots] - 1.0
     valid = wide >= 0.0
     slot = lax.broadcasted_iota(jnp.int32, (1, slots), 1)
     one = lax.broadcasted_iota(jnp.int32, (slots, slots), 0)

time: 57.6 us -> 57.5 us (level)
  no operation moved by 1% of the time
where the time goes in v5:
time: 57.5 us; the launch traced here: 57.1 us
  waiting for transfers between devices  23.4 us (41%)
  starting transfers between devices  23.3 us (41%)
  Pallas kernels  8.99 us (16%)
  between operations  1.36 us (2%)
    all_to_all x2, waiting for transfers between devices, exchange(): lax.all_to_all(rows.reshape(peers, count, 1, LANES), 'blk', split_axis=0,...  22.6 us
    all_to_all x2, starting transfers between devices, exchange(): lax.all_to_all(rows.reshape(peers, count, 1, LANES), 'blk', split_axis=0,...  18 us
    ppermute x2, starting transfers between devices, from_behind(): lax.ppermute(value, axis, [(source, source + steps) for source in range(f...  5.32 us
    pallas_call x1, Pallas kernels, per_device(): pl.pallas_call(main_kernel, name='pairs', compiler_params=limit(8), out_s...  5.18 us
    pallas_call x1, Pallas kernels, per_device(): pl.pallas_call(pack_kernel, name='pack', out_shape=(on_chip(peers * MSG,...  1.95 us
  transfers between devices with their start and end apart: 4, of which 3 were waited for; matrix products, arithmetic and copies ran while one was open for 0% of the time, Pallas kernels for 2%

profile of v5, /device:TPU:1, one launch (start us, length us, event | category | flops | bytes accessed | tf_op | source)
XLA Modules:
  0.0 57.1 jit_solution(6236818732550167715)
XLA Ops:
  1.3 2.0 %pack.1 = (f32[832,128]{1,0:T(8,128)}, f32[24,128]{1,0:T(8,128)S(1)}, s32[133]{0:T(256)S(4)}) custom-call(s32[64]{0:T(128)} %local_ref.2, s32[64]{0:T(128)} %peer_ref.1, s32[64]{0:T(128)} %shift_ref.1, s32[1]{0:T(128)S(6)} %copy.13.count_ref, s32[4]{0:T(128)} %face_ref.2, f32[3,2048]{1,0:T(4,128)} %pos_ref.3, f32[3,2048]{1,0:T(4,128)} %dir_ref.3), custom_call_target="tpu_custom_call" | custom-call | tf_op jit(solution)/shard_map/pack/pallas_call | solution.py:380
  3.2 0.0 copy-start
  3.2 0.0 copy-start.1
  3.2 11.7 %all-to-all-start = ((f32[64,13,1,128]{3,2,1,0:T(1,128)}), f32[64,13,1,128]{3,2,1,0:T(1,128)S(1)}, u32[]{:S(2)}, u32[]{:S(2)}) async-start(f32[64,13,1,128]{3,2,1,0:T(1,128)} %bitcast), calls=%async_computation | async-start | bytes 851968 | tf_op jit(solution)/shard_map/all_to_all | solution.py:362
  15.0 0.0 copy-start.2
  15.0 0.0 copy-start.3
  15.0 4.0 %collective-permute-start = (f32[24,128]{1,0:T(8,128)S(1)}, f32[24,128]{1,0:T(8,128)S(1)}, u32[]{:S(2)}, u32[]{:S(2)}) collective-permute-start(f32[24,128]{1,0:T(8,128)S(1)} %get-tuple-element.15), channel_id=1, source_target_pairs={{0,1},{1,2},{2,3},{3,4},{4,5},{5,6},{6,7},{8,9},{9,10},{10,11},{11... | collective-permute-start | bytes 36872 | tf_op jit(solution)/shard_map/ppermute | solution.py:29
  19.0 0.8 %collective-permute-done.incoming_ref = f32[24,128]{1,0:T(8,128)S(1)} collective-permute-done((f32[24,128]{1,0:T(8,128)S(1)}, f32[24,128]{1,0:T(8,128)S(1)}, u32[]{:S(2)}, u32[]{:S(2)}) %collective-permute-start) | collective-permute-done | bytes 12320 | tf_op jit(solution)/shard_map/ppermute | solution.py:29
  19.9 0.0 copy-done
  19.9 0.0 copy-done.1
  19.9 0.0 copy-done.2
  19.9 0.0 copy-done.3
  19.9 1.0 %cross.1 = (f32[16,8,256]{2,1,0:T(8,128)S(1)}, f32[24,128]{1,0:T(8,128)S(1)}, f32[16,8,128]{2,1,0:T(8,128)S(1)}, bf16[16,256,128]{2,1,0:T(8,128)(2,1)S(1)}, bf16...) custom-call(s32[8]{0:T(128)S(1)} %copy-done.2, s32[8]{0:T(128)S(1)} %copy-done.3, f32[3,2048]{1,0:T(4,128)S(1)} %copy-done, ...), custom_call_target="tpu_custom_call" | custom-call | tf_op jit(solution)/shard_map/cross/pallas_call | solution.py:397
  20.9 9.4 %all-to-all-done = f32[64,13,1,128]{3,2,1,0:T(1,128)S(1)} async-done(((f32[64,13,1,128]{3,2,1,0:T(1,128)}), f32[64,13,1,128]{3,2,1,0:T(1,128)S(1)}, u32[]{:S(2)}, u32[]{:S(2)}) %all-to-all-start) | async-done | bytes 426016 | tf_op jit(solution)/shard_map/all_to_all | solution.py:362
  30.3 5.2 %pairs.1 = (f32[768,128]{1,0:T(8,128)}, f32[16,8,128]{2,1,0:T(8,128)S(1)}) custom-call(f32[832,128]{1,0:T(8,128)S(1)} %bitcast.4, f32[16,8,256]{2,1,0:T(8,128)S(1)} %get-tuple-element.16.sums_in_ref, f32[16,8,128]{2,1,0:T(8,128)S(1)} %get-tuple-element.17.rows_ref, bf16[16,256,128]{2,1,0:T(8,128)(2,1)S(1)} %get-tuple-element.18.feature_ref, ...), custom_call_target="tpu_custom_call" | custom-call | tf_op jit(solution)/shard_map/pairs/pallas_call | solution.py:406
  35.4 6.2 %all-to-all-start.1 = ((f32[64,12,1,128]{3,2,1,0:T(1,128)}), f32[64,12,1,128]{3,2,1,0:T(1,128)S(1)}, u32[]{:S(2)}, u32[]{:S(2)}) async-start(f32[64,12,1,128]{3,2,1,0:T(1,128)} %bitcast.2), calls=%async_computation.1 | async-start | bytes 786432 | tf_op jit(solution)/shard_map/all_to_all | solution.py:362
  41.7 1.3 %collective-permute-start.1 = (f32[24,128]{1,0:T(8,128)S(1)}, f32[24,128]{1,0:T(8,128)S(1)}, u32[]{:S(2)}, u32[]{:S(2)}) collective-permute-start(f32[24,128]{1,0:T(8,128)S(1)} %get-tuple-element.23), channel_id=1, source_target_pairs={{1,0},{2,1},{3,2},{4,3},{5,4},{6,5},{7,6},{9,8},{10,9},{11,10},{12... | collective-permute-start | bytes 36872 | tf_op jit(solution)/shard_map/ppermute | solution.py:29
  43.0 13.2 %all-to-all-done.1 = f32[64,12,1,128]{3,2,1,0:T(1,128)S(1)} async-done(((f32[64,12,1,128]{3,2,1,0:T(1,128)}), f32[64,12,1,128]{3,2,1,0:T(1,128)S(1)}, u32[]{:S(2)}, u32[]{:S(2)}) %all-to-all-start.1) | async-done | bytes 393248 | tf_op jit(solution)/shard_map/all_to_all | solution.py:362
  56.2 0.2 gather.1.total_ref
  56.4 0.0 collective-permute-done.1.back_ref
  56.4 0.7 %finish.1 = (f32[3,2048]{1,0:T(4,128)}, f32[3,2048]{1,0:T(4,128)}) custom-call(s32[133]{0:T(256)S(4)} %get-tuple-element.13.plan_ref, f32[17,8,128]{2,1,0:T(8,128)S(1)} %gather.1.total_ref, f32[24,128]{1,0:T(8,128)S(1)} %collective-permute-done.1.back_ref), custom_call_target="tpu_custom_call" | custom-call | tf_op jit(solution)/shard_map/finish/pallas_call | solution.py:432
Async XLA Ops:
  3.2 16.6 %copy-start = (f32[3,2048]{1,0:T(4,128)S(1)}, f32[3,2048]{1,0:T(4,128)}, u32[]{:S(2)}) copy-start(f32[3,2048]{1,0:T(4,128)} %pos_ref.3) | copy-start | bytes 73732
  3.2 16.6 %copy-start.1 = (f32[3,2048]{1,0:T(4,128)S(1)}, f32[3,2048]{1,0:T(4,128)}, u32[]{:S(2)}) copy-start(f32[3,2048]{1,0:T(4,128)} %dir_ref.3) | copy-start | bytes 73732
  3.2 27.0 %all-to-all-start = ((f32[64,13,1,128]{3,2,1,0:T(1,128)}), f32[64,13,1,128]{3,2,1,0:T(1,128)S(1)}, u32[]{:S(2)}, u32[]{:S(2)}) async-start(f32[64,13,1,128]{3,2,1,0:T(1,128)} %bitcast), calls=%async_computation | async-start | bytes 851968 | tf_op jit(solution)/shard_map/all_to_all | solution.py:362
  15.0 4.9 %copy-start.2 = (s32[8]{0:T(128)S(1)}, s32[8]{0:T(128)}, u32[]{:S(2)}) copy-start(s32[8]{0:T(128)} %local_ref.3) | copy-start | bytes 100
  15.0 4.9 %copy-start.3 = (s32[8]{0:T(128)S(1)}, s32[8]{0:T(128)}, u32[]{:S(2)}) copy-start(s32[8]{0:T(128)} %face_ref.3) | copy-start | bytes 100
  15.0 4.9 %collective-permute-start = (f32[24,128]{1,0:T(8,128)S(1)}, f32[24,128]{1,0:T(8,128)S(1)}, u32[]{:S(2)}, u32[]{:S(2)}) collective-permute-start(f32[24,128]{1,0:T(8,128)S(1)} %get-tuple-element.15), channel_id=1, source_target_pairs={{0,1},{1,2},{2,3},{3,4},{4,5},{5,6},{6,7},{8,9},{9,10},{10,11},{11... | collective-permute-start | bytes 36872 | tf_op jit(solution)/shard_map/ppermute | solution.py:29
  35.4 20.8 %all-to-all-start.1 = ((f32[64,12,1,128]{3,2,1,0:T(1,128)}), f32[64,12,1,128]{3,2,1,0:T(1,128)S(1)}, u32[]{:S(2)}, u32[]{:S(2)}) async-start(f32[64,12,1,128]{3,2,1,0:T(1,128)} %bitcast.2), calls=%async_computation.1 | async-start | bytes 786432 | tf_op jit(solution)/shard_map/all_to_all | solution.py:362
  41.7 14.7 %collective-permute-start.1 = (f32[24,128]{1,0:T(8,128)S(1)}, f32[24,128]{1,0:T(8,128)S(1)}, u32[]{:S(2)}, u32[]{:S(2)}) collective-permute-start(f32[24,128]{1,0:T(8,128)S(1)} %get-tuple-element.23), channel_id=1, source_target_pairs={{1,0},{2,1},{3,2},{4,3},{5,4},{6,5},{7,6},{9,8},{10,9},{11,10},{12... | collective-permute-start | bytes 36872 | tf_op jit(solution)/shard_map/ppermute | solution.py:29
